TPU v7x, 1024 devices: a whole 4x4x32 slice. The times are simulated.
1024 devices in a mesh: context: 64 (over z, core), tensor: 16 (over x, y).
Axes of the slice: x: 4, y: 4, z: 32, core: 2. Of those that a mesh axis runs over, the one named last changes fastest.
Arguments:
- tokens: bfloat16 [16384, 4096], P(('context', 'tensor')), may hold values from -6 to 6
- norm_gain: float32 [4096], replicated, may hold values from 0.1 to 1.9
- w_qkv: bfloat16 [4096, 3, 4096], P(None, None, 'tensor'), may hold values from -0.09375 to 0.09375
- head_gain: float32 [4096], P('tensor'), may hold values from 0.1 to 1.9
- w_out: bfloat16 [4096, 4096], P('tensor'), may hold values from -0.09375 to 0.09375
Outputs:
- layer_out: bfloat16 [16384, 4096], P(('context', 'tensor'))
All inputs are finite; a program needn't handle non-finite values.
Results may differ from a plain program's by a relative error of at most 0.0088.
Values may be sent and summed in bfloat16 or wider, within the bound.
No kernel may reach another device: no remote copies, remote signals or barrier semaphores. Data moves between devices by JAX's collectives and lax.ppermute only.
A program may use at most 64 MiB of HBM per device.

v0:
```python
import jax
import jax.numpy as jnp
from jax import lax
from jax.sharding import PartitionSpec as P

HD = 128


def carried_in(value, axis, combine, identity):
    size, mine = (lax.axis_size(axis), lax.axis_index(axis))
    everything = lax.all_gather(value, axis)
    start = jnp.broadcast_to(jnp.asarray(identity, value.dtype), value.shape)

    def turn(k, before):
        reached = k < mine
        new = combine(before, everything[k])
        return jnp.where(reached, new, before)

    return lax.fori_loop(0, size, turn, start)


def norm_rows(rows, norm_gain):
    x32 = rows.astype(jnp.float32)
    scale = lax.rsqrt(jnp.mean(x32 * x32, axis=-1, keepdims=True) + 1e-05)
    return (x32 * scale * norm_gain).astype(jnp.bfloat16)


def add_states(earlier, later):
    return earlier + later


def local(tokens, norm_gain, w_qkv, head_gain, w_out):
    width = w_qkv.shape[0]
    local_heads = w_qkv.shape[2] // HD
    weight_flat = w_qkv.reshape(width, 3 * local_heads * HD)
    gathered = lax.all_gather(tokens, "tensor", axis=0, tiled=True)
    proj = jnp.dot(norm_rows(gathered, norm_gain), weight_flat, preferred_element_type=jnp.float32)
    block_rows = proj.shape[0]
    proj = proj.astype(jnp.bfloat16).reshape(block_rows, 3, local_heads, HD)
    query = proj[:, 0]
    keys = proj[:, 1]
    values = proj[:, 2]
    positions = lax.iota(jnp.int32, block_rows)
    causal = positions[:, None] >= positions[None, :]
    scores = jnp.einsum("thd,shd->hts", query, keys, preferred_element_type=jnp.float32)
    scores = jnp.where(causal[None], scores, 0.0).astype(jnp.bfloat16)
    intra = jnp.einsum("hts,shd->thd", scores, values, preferred_element_type=jnp.float32)
    block_state = jnp.einsum("thd,the->hde", keys, values, preferred_element_type=jnp.float32)
    prefix = carried_in(block_state, "context", add_states, jnp.zeros_like(block_state))
    inter = jnp.einsum(
        "thd,hde->the", query, prefix.astype(jnp.bfloat16), preferred_element_type=jnp.float32
    )
    attended = intra + inter
    scale = lax.rsqrt(jnp.mean(attended * attended, axis=-1, keepdims=True) + 1e-05)
    head_out = ((attended * scale).reshape(block_rows, local_heads * HD) * head_gain).astype(
        jnp.bfloat16
    )
    terms = jnp.dot(head_out, w_out, preferred_element_type=jnp.float32)
    summed = lax.psum_scatter(terms, "tensor", scatter_dimension=0, tiled=True)
    return (tokens.astype(jnp.float32) + summed).astype(jnp.bfloat16)


def solution(mesh):
    return jax.shard_map(
        local,
        mesh=mesh,
        in_specs=(
            P(("context", "tensor"), None),
            P(),
            P(None, None, "tensor"),
            P("tensor"),
            P("tensor", None),
        ),
        out_specs=P(("context", "tensor"), None),
        check_vma=False,
    )
```

profile of v0, /device:TPU:24, one launch (start us, length us, event | category | flops | bytes accessed | tf_op | source)
XLA Modules:
  0.0 429.3 jit_solution(16629954288429257684)
XLA Ops:
  7.3 8.7 %copy.17 = bf16[4096,3,256]{0,2,1:T(8,128)(2,1)} copy(bf16[4096,3,256]{2,0,1:T(8,128)(2,1)} %param.9) | data formatting | bytes 12582912 | tf_op args[2]
  16.1 83.1 %all-gather.4.cloned.1.call-done = bf16[256,4096]{1,0:T(8,128)(2,1)} async-done(((bf16[16,4096]{1,0:T(8,128)(2,1)}), bf16[256,4096]{1,0:T(8,128)(2,1)}) %all-gather.4.cloned.1.call-update) | async-done | bytes 2097168 | tf_op jit(solution)/shard_map/all_gather | solution.py:36
  99.2 2.1 fusion
  101.3 5.3 %fusion.7 = bf16[256,768]{1,0:T(8,128)(2,1)S(1)} fusion(bf16[4096,768]{0,1:T(8,128)(2,1)} %bitcast.32, bf16[256,4096]{1,0:T(8,128)(2,1)} %all-gather.4.cloned.1.call-done, f32[4096]{0:T(1024)S(1)} %copy-done.3, f32[256]{0:T(256)S(1)} %add_rsqrt_fusion.1), kind=kOutput, calls=%fused_computation.9 | convolution fusion | flops 1615003648 | bytes 8799232 | tf_op jit(solution)/shard_map/dot_general | solution.py:37
  108.5 142.6 %all-gather.6.cloned.1.call-done = f32[128,128,128]{2,1,0:T(8,128)} async-done(((f32[2,128,128]{2,1,0:T(8,128)}), f32[128,128,128]{2,1,0:T(8,128)}) %all-gather.6.cloned.1.call-update) | async-done | bytes 8388624 | tf_op jit(solution)/shard_map/all_gather | solution.py:11
  251.1 62.3 %while.14 = (s32[]{:T(128)}, f32[2,128,128]{2,1,0:T(8,128)S(1)}, s32[]{:T(128)}, f32[64,2,128,128]{3,2,1,0:T(8,128)}, s32[]{:T(128)}, /*index=5*/s32[]{:T(128)}) while((s32[]{:T(128)}, f32[2,128,128]{2,1,0:T(8,128)S(1)}, s32[]{:T(128)}, f32[64,2,128,128]{3,2,1,0:T(8,128)}, s32[]{:T(128)}, /*index=5*/s32[]{:T(128)}) %tuple.44), condition=%wide.region_2.3_spmd.clone, body=%wide.region_1.2_spmd.clone.sunk | while | flops 98308 | bytes 393309 | solution.py:19
  252.1 0.9 add_select_fusion.2
  253.0 0.9 add_select_fusion.2
  254.0 0.9 add_select_fusion.2
  255.0 0.9 add_select_fusion.2
  255.9 0.9 add_select_fusion.2
  256.9 0.9 add_select_fusion.2
  257.9 0.9 add_select_fusion.2
  258.9 0.9 add_select_fusion.2
  259.8 0.9 add_select_fusion.2
  260.8 0.9 add_select_fusion.2
  261.8 0.9 add_select_fusion.2
  262.8 0.9 add_select_fusion.2
  263.7 0.9 add_select_fusion.2
  264.7 0.9 add_select_fusion.2
  265.7 0.9 add_select_fusion.2
  313.8 2.7 fusion.22
  316.5 104.6 %reduce-scatter.2.cloned.1.call-done = f32[16,4096]{1,0:T(8,128)} async-done(((f32[256,4096]{1,0:T(8,128)}), f32[16,4096]{1,0:T(8,128)}) %reduce-scatter.2.cloned.1.call-update) | async-done | bytes 262160 | tf_op jit(solution)/shard_map/reduce_scatter | solution.py:59
  421.1 1.6 add_convert_fusion
  (75 shorter events, 49.5 us)
Async XLA Ops:
  6.5 307.3 %copy-start = (bf16[256,4096]{1,0:T(8,128)(2,1)S(1)}, bf16[256,4096]{1,0:T(8,128)(2,1)}, u32[]{:S(2)}) copy-start(bf16[256,4096]{1,0:T(8,128)(2,1)} %param.11) | copy-start | bytes 6291460
  6.5 92.6 %all-gather.4.cloned.1.call-start = ((), (), s32[]{:S(2)}) async-start(), calls=%async_computation.1 | async-start | bytes 2228224 | tf_op jit(solution)/shard_map/all_gather | solution.py:36
  7.3 94.0 %copy-start.3 = (f32[4096]{0:T(1024)S(1)}, f32[4096]{0:T(1024)}, u32[]{:S(2)}) copy-start(f32[4096]{0:T(1024)} %param.8) | copy-start | bytes 49156
  7.3 243.8 %all-gather.6.cloned.1.call-start = ((), (), s32[]{:S(2)}) async-start(), calls=%async_computation.3 | async-start | bytes 8519680 | tf_op jit(solution)/shard_map/all_gather | solution.py:11
  106.6 207.1 %copy-start.2 = (f32[256]{0:T(256)S(1)}, f32[256]{0:T(256)}, u32[]{:S(2)}) copy-start(f32[256]{0:T(256)} %param.10) | copy-start | bytes 3076
  108.0 313.1 %reduce-scatter.2.cloned.1.call-start = ((), (), s32[]{:S(2)}) async-start(), calls=%async_computation.2 | async-start | bytes 4456448 | tf_op jit(solution)/shard_map/reduce_scatter | solution.py:59
  313.8 107.3 %copy-start.1 = (bf16[16,4096]{1,0:T(8,128)(2,1)S(1)}, bf16[16,4096]{1,0:T(8,128)(2,1)}, u32[]{:S(2)}) copy-start(bf16[16,4096]{1,0:T(8,128)(2,1)} %param.7) | copy-start | bytes 393220
Sparse Core Ops, SparseCore 0:
  11.5 87.6 all-gather.3
  108.1 142.9 all-gather.5
  316.6 104.4 reduce-scatter.1
where the time goes:
time: 431 us; the launch traced here: 429 us
  waiting for transfers between devices  331 us (77%)
  other arithmetic  64.7 us (15%)
  between operations  13.2 us (3%)
  matrix products  9.47 us (2%)
  local copies, waits for them, and re-layouts  9.24 us (2%)
    all_gather x1, waiting for transfers between devices, carried_in(): everything = lax.all_gather(value, axis)  143 us
    reduce_scatter x1, waiting for transfers between devices, local(): summed = lax.psum_scatter(terms, 'tensor', scatter_dimension=0, tiled=True)  105 us
    all_gather x1, waiting for transfers between devices, local(): gathered = lax.all_gather(tokens, 'tensor', axis=0, tiled=True)  83.1 us
    select_n x64, other arithmetic, turn(): return jnp.where(reached, new, before)  60.8 us
    unnamed x10, local copies, waits for them, and re-layouts  8.88 us
  transfers between devices with their start and end apart: 3, of which 3 were waited for; matrix products, arithmetic and copies ran while one was open for 2% of the time, Pallas kernels for 0%

commit v1 on v0

v1 whole, which is shorter than its diff:
```python
import jax
import jax.numpy as jnp
from jax import lax
from jax.sharding import Mesh
from jax.sharding import PartitionSpec as P

HD = 128
SIDE = 4
NEAR = 4
PLANE = ("core", "x", "y")
ALL = ("zh", "zl", "core", "x", "y")


def spot(core, bx, by, px, py):
    x, y = (core + 2 * bx + px) % SIDE, (core + 2 * by + py) % SIDE
    return core * SIDE * SIDE + x * SIDE + y


BITS = [(a, b) for a in range(2) for b in range(2)]
SQUARES = [[spot(c, bx, by, px, py) for px, py in BITS] for c in range(2) for bx, by in BITS]
CROSSES = [
    [spot(c, bx, by, (bx + jx) % 2, (by + jy) % 2) for bx, by in BITS]
    for c in range(2)
    for jx, jy in BITS
]


def swap(value, axes, groups=None):
    return lax.all_to_all(
        value, axes, split_axis=0, concat_axis=0, tiled=True, axis_index_groups=groups
    )


def norm_rows(rows, norm_gain):
    x32 = rows.astype(jnp.float32)
    scale = lax.rsqrt(jnp.mean(x32 * x32, axis=-1, keepdims=True) + 1e-05)
    return (x32 * scale * norm_gain).astype(jnp.bfloat16)


def gather_rows(rows):
    n, width = rows.shape
    for groups in (SQUARES, CROSSES):
        copies = jnp.broadcast_to(rows[None], (4,) + rows.shape)
        rows = swap(copies, PLANE, groups).reshape(4 * rows.shape[0], width)
    return rows


def scatter_sum(terms):
    for groups in (CROSSES, SQUARES):
        parts = terms.astype(jnp.bfloat16).reshape(4, terms.shape[0] // 4, terms.shape[1])
        parts = swap(parts, PLANE, groups).astype(jnp.float32)
        terms = (parts[0] + parts[1]) + (parts[2] + parts[3])
    return terms


def row_places(count):
    part = count // (SIDE * SIDE)
    i = lax.iota(jnp.int32, count)
    core = lax.axis_index("core")
    slot = i // part
    bx, by, px, py = slot // 8, slot // 4 % 2, slot // 2 % 2, slot % 2
    x, y = (core + 2 * bx + px) % SIDE, (core + 2 * by + py) % SIDE
    return (x * SIDE + y) * part + i % part


def earlier_sum(state):
    members = lax.axis_size("zl") * lax.axis_size("core")
    far = lax.axis_size("zh")
    shape = state.shape
    cut = swap(state.reshape(members, -1, HD), ("zl", "core"))
    before = [jnp.zeros_like(cut[0])]
    for m in range(members):
        before.append(before[-1] + cut[m])
    total = before.pop().astype(jnp.bfloat16)
    totals = swap(jnp.broadcast_to(total[None], (far,) + total.shape), ("zh",))
    mine = lax.axis_index("zh")
    reached = lax.broadcasted_iota(jnp.int32, (far, 1, 1), 0) < mine
    base = jnp.sum(jnp.where(reached, totals.astype(jnp.float32), 0.0), axis=0)
    prefix = jnp.stack([b + base for b in before]).astype(jnp.bfloat16)
    return swap(prefix, ("zl", "core")).reshape(shape)


def local(tokens, norm_gain, w_qkv, head_gain, w_out):
    heads = w_qkv.shape[2] // HD
    gathered = gather_rows(norm_rows(tokens, norm_gain))
    rows = gathered.shape[0]
    proj = [
        jnp.dot(gathered, w_qkv[:, j], preferred_element_type=jnp.float32).astype(jnp.bfloat16)
        for j in range(3)
    ]
    query, keys, values = [[p[:, h * HD : (h + 1) * HD] for h in range(heads)] for p in proj]
    state = jnp.stack(
        [
            jnp.einsum("td,te->de", k, v, preferred_element_type=jnp.float32)
            for k, v in zip(keys, values)
        ]
    )
    prefix = earlier_sum(state)
    place = row_places(rows)
    causal = place[:, None] >= place[None, :]
    outs = []
    for h in range(heads):
        scores = jnp.einsum("td,sd->ts", query[h], keys[h], preferred_element_type=jnp.float32)
        scores = jnp.where(causal, scores, 0.0).astype(jnp.bfloat16)
        attended = jnp.dot(scores, values[h], preferred_element_type=jnp.float32) + jnp.dot(
            query[h], prefix[h], preferred_element_type=jnp.float32
        )
        scale = lax.rsqrt(jnp.mean(attended * attended, axis=-1, keepdims=True) + 1e-05)
        gain = head_gain[h * HD : (h + 1) * HD]
        outs.append((attended * scale * gain).astype(jnp.bfloat16))
    head_out = jnp.concatenate(outs, axis=1)
    terms = jnp.dot(head_out, w_out, preferred_element_type=jnp.float32)
    return (tokens.astype(jnp.float32) + scatter_sum(terms)).astype(jnp.bfloat16)


def solution(mesh):
    context = mesh.shape["context"]
    cut = Mesh(mesh.devices.reshape(context // (2 * NEAR), NEAR, 2, SIDE, SIDE), ALL)
    return jax.shard_map(
        local,
        mesh=cut,
        in_specs=(
            P(ALL, None),
            P(),
            P(None, None, ("x", "y")),
            P(("x", "y")),
            P(("x", "y"), None),
        ),
        out_specs=P(ALL, None),
        check_vma=False,
    )
```

time: 431 us -> 150 us (0.35)
  waiting for transfers between devices: 331 us -> 27.2 us
  blocking collectives: 0 us -> 82.3 us
  other arithmetic: 64.7 us -> 8.77 us
  starting transfers between devices: 0.08 us -> 20.5 us
  between operations: 13.2 us -> 0.18 us
  local copies, waits for them, and re-layouts: 9.24 us -> 1.54 us
    all_gather x2 -> x0, waiting for transfers between devices: 226 us -> none  [the longest x1 143 us: carried_in(): everything = lax.all_gather(value, axis)]
    reduce_scatter x1 -> x0, waiting for transfers between devices: 105 us -> none  [local(): summed = lax.psum_scatter(terms, 'tensor', scatter_dimension=0, tiled=True)]
    all_to_all x0 -> x5, blocking collectives: none -> 82.3 us  [swap(): lax.all_to_all(value, axes, split_axis=0, concat_axis=0, tiled=True, axis...]
    select_n x64 -> x0, other arithmetic: 60.8 us -> none  [turn(): return jnp.where(reached, new, before)]
    all_to_all x0 -> x2, waiting for transfers between devices: none -> 27.2 us  [swap(): lax.all_to_all(value, axes, split_axis=0, concat_axis=0, tiled=True, axis...]
    all_to_all x0 -> x2, starting transfers between devices: none -> 20.5 us  [swap(): lax.all_to_all(value, axes, split_axis=0, concat_axis=0, tiled=True, axis...]
    unnamed x10, local copies, waits for them, and re-layouts: 8.88 us -> 0.61 us
  transfers between devices with their start and end apart: 3 -> 2, of which waited for: 3 -> 2; matrix products, arithmetic and copies ran while one was open for 2% -> 2% of each run, Pallas kernels for 0% -> 0%
where the time goes in v1:
time: 150 us; the launch traced here: 147 us
  blocking collectives  82.3 us (55%)
  waiting for transfers between devices  27.2 us (18%)
  starting transfers between devices  20.5 us (14%)
  other arithmetic  8.77 us (6%)
  matrix products  6.69 us (4%)
  local copies, waits for them, and re-layouts  1.54 us (1%)
    all_to_all x5, blocking collectives, swap(): lax.all_to_all(value, axes, split_axis=0, concat_axis=0, tiled=True, axis...  82.3 us
    all_to_all x2, waiting for transfers between devices, swap(): lax.all_to_all(value, axes, split_axis=0, concat_axis=0, tiled=True, axis...  27.2 us
    all_to_all x2, starting transfers between devices, swap(): lax.all_to_all(value, axes, split_axis=0, concat_axis=0, tiled=True, axis...  20.5 us
    dot_general x3, matrix products, local(): jnp.dot(gathered, w_qkv[:, j], preferred_element_type=jnp.float32)  4.38 us
    unnamed x7, other arithmetic  4.22 us
  transfers between devices with their start and end apart: 2, of which 2 were waited for; matrix products, arithmetic and copies ran while one was open for 2% of the time, Pallas kernels for 0%

profile of v1, /device:TPU:24, one launch (start us, length us, event | category | flops | bytes accessed | tf_op | source)
XLA Modules:
  0.0 147.2 jit_solution(1396571740090546323)
XLA Ops:
  0.0 1.2 fusion.28
  1.2 1.0 fusion.30
  2.3 10.0 %all_to_all.35 = bf16[4,16,4096]{2,1,0:T(8,128)(2,1)S(1)} all-to-all(bf16[4,16,4096]{2,1,0:T(8,128)(2,1)S(1)} %broadcast_in_dim.27), channel_id=1, replica_groups={{0,1,4,5},{2,3,6,7},{8,9,12,13},{10,11,14,15},{21,22,25,26},{23,20,27,2..., dimensions={0} | all-to-all | bytes 1048576 | tf_op jit(solution)/shard_map/all_to_all | solution.py:29
  12.6 33.5 %all_to_all.36 = bf16[4,64,4096]{2,1,0:T(8,128)(2,1)S(1)} all-to-all(bf16[4,64,4096]{2,1,0:T(8,128)(2,1)S(1)} %broadcast_in_dim.48), channel_id=1, replica_groups={{0,3,12,15},{1,2,13,14},{4,7,8,11},{5,6,9,10},{21,20,17,16},{22,23,18,1..., dimensions={0} | all-to-all | bytes 4194304 | tf_op jit(solution)/shard_map/all_to_all | solution.py:29
  46.0 0.7 fusion.17
  47.4 0.7 fusion.14
  48.5 9.1 %all_to_all.37 = f32[8,32,128]{2,1,0:T(8,128)S(1)} all-to-all(f32[8,32,128]{2,1,0:T(8,128)S(1)} %bitcast.83), channel_id=1, replica_groups=mesh['zh'=8,'zl'=4,'core'=2,'x'=4,'y'=4] {'zl','core'}, dimensions={0} | all-to-all | bytes 262144 | tf_op jit(solution)/shard_map/all_to_all | solution.py:29
  57.7 0.6 broadcast_in_dim.52
  58.3 17.0 %all-to-all-start.3 = ((bf16[8,32,128]{2,1,0:T(8,128)(2,1)}), bf16[8,32,128]{2,1,0:T(8,128)(2,1)S(1)}, u32[]{:S(2)}, u32[]{:S(2)}) async-start(bf16[8,32,128]{2,1,0:T(8,128)(2,1)} %broadcast_in_dim.52), calls=%async_computation.3 | async-start | bytes 131072 | tf_op jit(solution)/shard_map/all_to_all | solution.py:29
  75.3 24.2 %all-to-all-done.3 = bf16[8,32,128]{2,1,0:T(8,128)(2,1)S(1)} async-done(((bf16[8,32,128]{2,1,0:T(8,128)(2,1)}), bf16[8,32,128]{2,1,0:T(8,128)(2,1)S(1)}, u32[]{:S(2)}, u32[]{:S(2)}) %all-to-all-start.3) | async-done | bytes 65568 | tf_op jit(solution)/shard_map/all_to_all | solution.py:29
  100.2 0.6 constant_dynamic-update-slice_fusion.6
  100.8 0.6 constant_dynamic-update-slice_fusion.5
  101.4 0.6 constant_dynamic-update-slice_fusion.4
  102.0 0.6 constant_dynamic-update-slice_fusion.3
  102.6 0.6 constant_dynamic-update-slice_fusion.2
  103.3 0.6 constant_dynamic-update-slice_fusion.1
  103.9 0.6 constant_dynamic-update-slice_fusion
  104.5 3.5 %all-to-all-start.4 = ((bf16[8,32,128]{2,1,0:T(8,128)(2,1)}), bf16[8,32,128]{2,1,0:T(8,128)(2,1)S(1)}, u32[]{:S(2)}, u32[]{:S(2)}) async-start(bf16[8,32,128]{2,1,0:T(8,128)(2,1)} %constant_dynamic-update-slice_fusion), calls=%async_computation.4 | async-start | bytes 131072 | tf_op jit(solution)/shard_map/all_to_all | solution.py:29
  108.0 2.9 %fusion.11 = bf16[256,256]{1,0:T(8,128)(2,1)S(1)} fusion(bf16[256,4096]{1,0:T(8,128)(2,1)} %bitcast.82, bf16[4096,3,256]{2,0,1:T(8,128)(2,1)} %param.7), kind=kOutput, calls=%fused_computation.14 | convolution fusion | flops 536936448 | bytes 4325376 | tf_op jit(solution)/shard_map/dot_general | solution.py:88
  110.9 3.0 %all-to-all-done.4 = bf16[8,32,128]{2,1,0:T(8,128)(2,1)S(1)} async-done(((bf16[8,32,128]{2,1,0:T(8,128)(2,1)}), bf16[8,32,128]{2,1,0:T(8,128)(2,1)S(1)}, u32[]{:S(2)}, u32[]{:S(2)}) %all-to-all-start.4) | async-done | bytes 65568 | tf_op jit(solution)/shard_map/all_to_all | solution.py:29
  115.2 0.7 convolution_convert_fusion
  116.0 20.4 %all_to_all.38 = bf16[4,64,4096]{2,1,0:T(8,128)(2,1)S(1)} all-to-all(bf16[4,64,4096]{2,1,0:T(8,128)(2,1)S(1)} %bitcast.77), channel_id=1, replica_groups={{0,3,12,15},{1,2,13,14},{4,7,8,11},{5,6,9,10},{21,20,17,16},{22,23,18,1..., dimensions={0} | all-to-all | bytes 4194304 | tf_op jit(solution)/shard_map/all_to_all | solution.py:29
  137.1 9.2 %all_to_all.39 = bf16[4,16,4096]{2,1,0:T(8,128)(2,1)S(1)} all-to-all(bf16[4,16,4096]{2,1,0:T(8,128)(2,1)S(1)} %bitcast.79), channel_id=1, replica_groups={{0,1,4,5},{2,3,6,7},{8,9,12,13},{10,11,14,15},{21,22,25,26},{23,20,27,2..., dimensions={0} | all-to-all | bytes 1048576 | tf_op jit(solution)/shard_map/all_to_all | solution.py:29
  146.5 0.7 fusion.31
  (33 shorter events, 4.1 us)
Async XLA Ops:
  0.0 115.2 %copy-start = (bf16[256,4096]{1,0:T(8,128)(2,1)S(1)}, bf16[256,4096]{1,0:T(8,128)(2,1)}, u32[]{:S(2)}) copy-start(bf16[256,4096]{1,0:T(8,128)(2,1)} %param.9) | copy-start | bytes 6291460
  12.3 33.7 %copy-start.4 = (bf16[4096,3,256]{2,0,1:T(8,128)(2,1)S(1)}, bf16[4096,3,256]{2,0,1:T(8,128)(2,1)}, u32[]{:S(2)}) copy-start(bf16[4096,3,256]{2,0,1:T(8,128)(2,1)} %param.7) | copy-start | bytes 18874372
  46.0 1.3 copy-start.1
  47.3 27.9 %copy-start.3 = (f32[256]{0:T(256)S(1)}, f32[256]{0:T(256)}, u32[]{:S(2)}) copy-start(f32[256]{0:T(256)} %param.8) | copy-start | bytes 3076
  58.3 41.2 %all-to-all-start.3 = ((bf16[8,32,128]{2,1,0:T(8,128)(2,1)}), bf16[8,32,128]{2,1,0:T(8,128)(2,1)S(1)}, u32[]{:S(2)}, u32[]{:S(2)}) async-start(bf16[8,32,128]{2,1,0:T(8,128)(2,1)} %broadcast_in_dim.52), calls=%async_computation.3 | async-start | bytes 131072 | tf_op jit(solution)/shard_map/all_to_all | solution.py:29
  104.5 9.4 %all-to-all-start.4 = ((bf16[8,32,128]{2,1,0:T(8,128)(2,1)}), bf16[8,32,128]{2,1,0:T(8,128)(2,1)S(1)}, u32[]{:S(2)}, u32[]{:S(2)}) async-start(bf16[8,32,128]{2,1,0:T(8,128)(2,1)} %constant_dynamic-update-slice_fusion), calls=%async_computation.4 | async-start | bytes 131072 | tf_op jit(solution)/shard_map/all_to_all | solution.py:29
  137.1 9.3 %copy-start.2 = (bf16[16,4096]{1,0:T(8,128)(2,1)S(1)}, bf16[16,4096]{1,0:T(8,128)(2,1)}, u32[]{:S(2)}) copy-start(bf16[16,4096]{1,0:T(8,128)(2,1)} %param.5) | copy-start | bytes 393220

commit v2 on v1

--- a/solution.py
+++ b/solution.py
@@ -1,6 +1,8 @@
 import jax
 import jax.numpy as jnp
 from jax import lax
+from jax.experimental import pallas as pl
+from jax.experimental.pallas import tpu as pltpu
 from jax.sharding import Mesh
 from jax.sharding import PartitionSpec as P
 
@@ -31,25 +33,36 @@
     )
 
 
-def norm_rows(rows, norm_gain):
-    x32 = rows.astype(jnp.float32)
+def norm_kernel(rows_ref, gain_ref, out_ref):
+    x32 = rows_ref[...].astype(jnp.float32)
     scale = lax.rsqrt(jnp.mean(x32 * x32, axis=-1, keepdims=True) + 1e-05)
-    return (x32 * scale * norm_gain).astype(jnp.bfloat16)
+    normed = (x32 * scale * gain_ref[...]).astype(jnp.bfloat16)
+    for i in range(out_ref.shape[0]):
+        out_ref[i] = normed
 
 
-def gather_rows(rows):
-    n, width = rows.shape
-    for groups in (SQUARES, CROSSES):
-        copies = jnp.broadcast_to(rows[None], (4,) + rows.shape)
-        rows = swap(copies, PLANE, groups).reshape(4 * rows.shape[0], width)
-    return rows
+def norm_copies(rows, norm_gain):
+    return pl.pallas_call(
+        norm_kernel,
+        out_shape=jax.ShapeDtypeStruct((4,) + rows.shape, jnp.bfloat16),
+        in_specs=[pl.BlockSpec(memory_space=pltpu.VMEM)] * 2,
+        out_specs=pl.BlockSpec(memory_space=pltpu.VMEM),
+        name="norm_copies",
+    )(rows, norm_gain[None])
+
+
+def gather_rows(copies):
+    width = copies.shape[2]
+    rows = swap(copies, PLANE, SQUARES).reshape(-1, width)
+    copies = jnp.broadcast_to(rows[None], (4,) + rows.shape)
+    return swap(copies, PLANE, CROSSES).reshape(-1, width)
 
 
 def scatter_sum(terms):
     for groups in (CROSSES, SQUARES):
         parts = terms.astype(jnp.bfloat16).reshape(4, terms.shape[0] // 4, terms.shape[1])
-        parts = swap(parts, PLANE, groups).astype(jnp.float32)
-        terms = (parts[0] + parts[1]) + (parts[2] + parts[3])
+        a, b, c, d = [p.astype(jnp.float32) for p in swap(parts, PLANE, groups)]
+        terms = (a + b) + (c + d)
     return terms
 
 
@@ -63,31 +76,40 @@
     return (x * SIDE + y) * part + i % part
 
 
-def earlier_sum(state):
-    members = lax.axis_size("zl") * lax.axis_size("core")
-    far = lax.axis_size("zh")
-    shape = state.shape
+def earlier_masks():
+    far, members = lax.axis_size("zh"), lax.axis_size("zl") * lax.axis_size("core")
+    group = lax.broadcasted_iota(jnp.int32, (far, 1, HD), 0)
+    to = lax.broadcasted_iota(jnp.int32, (members, members, 1, HD), 0)
+    since = lax.broadcasted_iota(jnp.int32, (members, members, 1, HD), 1)
+    return (group < lax.axis_index("zh")).astype(jnp.float32), (since < to).astype(jnp.float32)
+
+
+def earlier_sum(state, reached, lower):
+    shape, far, members = state.shape, reached.shape[0], lower.shape[0]
     cut = swap(state.reshape(members, -1, HD), ("zl", "core"))
-    before = [jnp.zeros_like(cut[0])]
-    for m in range(members):
-        before.append(before[-1] + cut[m])
-    total = before.pop().astype(jnp.bfloat16)
+    total = jnp.sum(cut, axis=0).astype(jnp.bfloat16)
+    before = jnp.sum(lower * cut[None], axis=1)
+    before, total = lax.optimization_barrier((before, total))
     totals = swap(jnp.broadcast_to(total[None], (far,) + total.shape), ("zh",))
-    mine = lax.axis_index("zh")
-    reached = lax.broadcasted_iota(jnp.int32, (far, 1, 1), 0) < mine
-    base = jnp.sum(jnp.where(reached, totals.astype(jnp.float32), 0.0), axis=0)
-    prefix = jnp.stack([b + base for b in before]).astype(jnp.bfloat16)
+    base = jnp.sum(reached * totals.astype(jnp.float32), axis=0)
+    prefix = (before + base).astype(jnp.bfloat16)
     return swap(prefix, ("zl", "core")).reshape(shape)
 
 
 def local(tokens, norm_gain, w_qkv, head_gain, w_out):
     heads = w_qkv.shape[2] // HD
-    gathered = gather_rows(norm_rows(tokens, norm_gain))
-    rows = gathered.shape[0]
+    reached, lower = earlier_masks()
+    place = row_places(tokens.shape[0] * SIDE * SIDE)
+    gains = [head_gain[h * HD : (h + 1) * HD] for h in range(heads)]
+    copies, reached, lower, place, gains = lax.optimization_barrier(
+        (norm_copies(tokens, norm_gain), reached, lower, place, gains)
+    )
+    gathered = gather_rows(copies)
     proj = [
         jnp.dot(gathered, w_qkv[:, j], preferred_element_type=jnp.float32).astype(jnp.bfloat16)
         for j in range(3)
     ]
+    proj = lax.optimization_barrier(proj)
     query, keys, values = [[p[:, h * HD : (h + 1) * HD] for h in range(heads)] for p in proj]
     state = jnp.stack(
         [
@@ -95,8 +117,7 @@
             for k, v in zip(keys, values)
         ]
     )
-    prefix = earlier_sum(state)
-    place = row_places(rows)
+    prefix = earlier_sum(state, reached, lower)
     causal = place[:, None] >= place[None, :]
     outs = []
     for h in range(heads):
@@ -106,8 +127,7 @@
             query[h], prefix[h], preferred_element_type=jnp.float32
         )
         scale = lax.rsqrt(jnp.mean(attended * attended, axis=-1, keepdims=True) + 1e-05)
-        gain = head_gain[h * HD : (h + 1) * HD]
-        outs.append((attended * scale * gain).astype(jnp.bfloat16))
+        outs.append((attended * scale * gains[h]).astype(jnp.bfloat16))
     head_out = jnp.concatenate(outs, axis=1)
     terms = jnp.dot(head_out, w_out, preferred_element_type=jnp.float32)
     return (tokens.astype(jnp.float32) + scatter_sum(terms)).astype(jnp.bfloat16)

time: 150 us -> 144 us (0.960)
  blocking collectives: 82.3 us -> 133 us
  waiting for transfers between devices: 27.2 us -> 0 us
  starting transfers between devices: 20.5 us -> 0 us
  other arithmetic: 8.77 us -> 1.29 us
  matrix products: 6.69 us -> 4.48 us
  Pallas kernels: 0 us -> 1.86 us
    all_to_all x5 -> x7, blocking collectives: 82.3 us -> 133 us  [swap(): lax.all_to_all(value, axes, split_axis=0, concat_axis=0, tiled=True, axis...]
    all_to_all x2 -> x0, waiting for transfers between devices: 27.2 us -> none  [swap(): lax.all_to_all(value, axes, split_axis=0, concat_axis=0, tiled=True, axis...]
    all_to_all x2 -> x0, starting transfers between devices: 20.5 us -> none  [swap(): lax.all_to_all(value, axes, split_axis=0, concat_axis=0, tiled=True, axis...]
    unnamed x7 -> x0, other arithmetic: 4.22 us -> none
    dot_general x3, matrix products: 4.38 us -> 2.17 us  [local(): jnp.dot(gathered, w_qkv[:, j], preferred_element_type=jnp.float32)]
    pallas_call x0 -> x1, Pallas kernels: none -> 1.86 us  [norm_copies(): pl.pallas_call(norm_kernel, out_shape=jax.ShapeDtypeStruct((4,) + rows.sh...]
    convert_element_type x4, other arithmetic: 1.67 us -> 0.13 us  [the longest x1 0.1 us: local(): outs.append((attended * scale * gains[h]).astype(jnp.bfloat16))]
  transfers between devices with their start and end apart: 2 -> 0, of which waited for: 2 -> 0; matrix products, arithmetic and copies ran while one was open for 2% -> 0% of each run, Pallas kernels for 0% -> 0%
where the time goes in v2:
time: 144 us; the launch traced here: 142 us
  blocking collectives  133 us (92%)
  matrix products  4.48 us (3%)
  Pallas kernels  1.86 us (1%)
    all_to_all x7, blocking collectives, swap(): lax.all_to_all(value, axes, split_axis=0, concat_axis=0, tiled=True, axis...  133 us

profile of v2, /device:TPU:24, one launch (start us, length us, event | category | flops | bytes accessed | tf_op | source)
XLA Modules:
  0.0 141.9 jit_solution(13103652505467249269)
XLA Ops:
  0.1 0.8 fusion.72
  0.9 1.9 %norm_copies.1 = bf16[4,16,4096]{2,1,0:T(8,128)(2,1)} custom-call(bf16[16,4096]{1,0:T(8,128)(2,1)} %rows_ref.1, f32[1,4096]{1,0:T(1,128)} %bitcast.50), custom_call_target="tpu_custom_call" | custom-call | tf_op jit(solution)/shard_map/norm_copies/pallas_call | solution.py:45
  2.8 10.2 %all_to_all.35 = bf16[4,16,4096]{2,1,0:T(8,128)(2,1)S(1)} all-to-all(bf16[4,16,4096]{2,1,0:T(8,128)(2,1)} %norm_copies.1), channel_id=1, replica_groups={{0,1,4,5},{2,3,6,7},{8,9,12,13},{10,11,14,15},{21,22,25,26},{23,20,27,2..., dimensions={0} | all-to-all | bytes 1048576 | tf_op jit(solution)/shard_map/all_to_all | solution.py:31
  13.1 0.2 broadcast_in_dim.15
  13.3 34.3 %all_to_all.36 = bf16[4,64,4096]{2,1,0:T(8,128)(2,1)S(1)} all-to-all(bf16[4,64,4096]{2,1,0:T(8,128)(2,1)S(1)} %broadcast_in_dim.15), channel_id=1, replica_groups={{0,3,12,15},{1,2,13,14},{4,7,8,11},{5,6,9,10},{21,20,17,16},{22,23,18,1..., dimensions={0} | all-to-all | bytes 4194304 | tf_op jit(solution)/shard_map/all_to_all | solution.py:31
  47.6 0.7 fusion.17
  48.3 0.7 fusion.14
  49.1 0.7 fusion.11
  49.8 0.2 convolution_bitcast_fusion.1
  50.0 0.2 convolution_bitcast_fusion
  50.2 9.1 %all_to_all.37 = f32[8,32,128]{2,1,0:T(8,128)S(1)} all-to-all(f32[8,32,128]{2,1,0:T(8,128)S(1)} %bitcast.45), channel_id=1, replica_groups=mesh['zh'=8,'zl'=4,'core'=2,'x'=4,'y'=4] {'zl','core'}, dimensions={0} | all-to-all | bytes 262144 | tf_op jit(solution)/shard_map/all_to_all | solution.py:31
  59.4 0.1 multiply_reduce_fusion
  59.5 40.5 %all_to_all.38 = bf16[8,32,128]{2,1,0:T(8,128)(2,1)S(1)} all-to-all(bf16[8,32,128]{2,1,0:T(8,128)(2,1)S(1)} %broadcast_in_dim.17), channel_id=1, replica_groups=mesh['zh'=8,'zl'=4,'core'=2,'x'=4,'y'=4] {'zh'}, dimensions={0} | all-to-all | bytes 131072 | tf_op jit(solution)/shard_map/all_to_all | solution.py:31
  100.0 9.2 %all_to_all.39 = bf16[8,32,128]{2,1,0:T(8,128)(2,1)S(1)} all-to-all(bf16[8,32,128]{2,1,0:T(8,128)(2,1)S(1)} %add_convert_fusion.1), channel_id=1, replica_groups=mesh['zh'=8,'zl'=4,'core'=2,'x'=4,'y'=4] {'zl','core'}, dimensions={0} | all-to-all | bytes 131072 | tf_op jit(solution)/shard_map/all_to_all | solution.py:31
  109.2 0.2 fusion.36
  109.4 0.4 multiply_reduce_fusion.1
  109.8 0.2 fusion.50
  110.0 0.4 multiply_reduce_fusion.2
  110.4 0.1 multiply_convert_fusion
  110.6 0.7 convolution_convert_fusion
  111.3 20.4 %all_to_all.40 = bf16[4,64,4096]{2,1,0:T(8,128)(2,1)S(1)} all-to-all(bf16[4,64,4096]{2,1,0:T(8,128)(2,1)S(1)} %bitcast.39), channel_id=1, replica_groups={{0,3,12,15},{1,2,13,14},{4,7,8,11},{5,6,9,10},{21,20,17,16},{22,23,18,1..., dimensions={0} | all-to-all | bytes 4194304 | tf_op jit(solution)/shard_map/all_to_all | solution.py:31
  131.7 0.3 add_convert_fusion
  132.0 9.1 %all_to_all.41 = bf16[4,16,4096]{2,1,0:T(8,128)(2,1)S(1)} all-to-all(bf16[4,16,4096]{2,1,0:T(8,128)(2,1)S(1)} %bitcast.41), channel_id=1, replica_groups={{0,1,4,5},{2,3,6,7},{8,9,12,13},{10,11,14,15},{21,22,25,26},{23,20,27,2..., dimensions={0} | all-to-all | bytes 1048576 | tf_op jit(solution)/shard_map/all_to_all | solution.py:31
  141.1 0.7 fusion.26
  (18 shorter events, 0.2 us)
Async XLA Ops:
  0.0 110.5 %copy-start = (bf16[256,4096]{1,0:T(8,128)(2,1)S(1)}, bf16[256,4096]{1,0:T(8,128)(2,1)}, u32[]{:S(2)}) copy-start(bf16[256,4096]{1,0:T(8,128)(2,1)} %param.9) | copy-start | bytes 6291460
  13.1 34.5 %copy-start.2 = (bf16[4096,3,256]{2,0,1:T(8,128)(2,1)S(1)}, bf16[4096,3,256]{2,0,1:T(8,128)(2,1)}, u32[]{:S(2)}) copy-start(bf16[4096,3,256]{2,0,1:T(8,128)(2,1)} %param.7) | copy-start | bytes 18874372
  131.7 9.4 %copy-start.1 = (bf16[16,4096]{1,0:T(8,128)(2,1)S(1)}, bf16[16,4096]{1,0:T(8,128)(2,1)}, u32[]{:S(2)}) copy-start(bf16[16,4096]{1,0:T(8,128)(2,1)} %rows_ref.1) | copy-start | bytes 393220

commit v3 on v2

--- a/solution.py
+++ b/solution.py
@@ -26,6 +26,8 @@
     for jx, jy in BITS
 ]
 
+WHOLE = [[spot(c, *far, *near) for far in BITS for near in BITS] for c in range(2)]
+
 
 def swap(value, axes, groups=None):
     return lax.all_to_all(
@@ -36,34 +38,33 @@
 def norm_kernel(rows_ref, gain_ref, out_ref):
     x32 = rows_ref[...].astype(jnp.float32)
     scale = lax.rsqrt(jnp.mean(x32 * x32, axis=-1, keepdims=True) + 1e-05)
-    normed = (x32 * scale * gain_ref[...]).astype(jnp.bfloat16)
-    for i in range(out_ref.shape[0]):
-        out_ref[i] = normed
+    out_ref[...] = (x32 * scale * gain_ref[...]).astype(jnp.bfloat16)
 
 
-def norm_copies(rows, norm_gain):
+def norm_rows(rows, norm_gain):
     return pl.pallas_call(
         norm_kernel,
-        out_shape=jax.ShapeDtypeStruct((4,) + rows.shape, jnp.bfloat16),
+        out_shape=jax.ShapeDtypeStruct(rows.shape, jnp.bfloat16),
         in_specs=[pl.BlockSpec(memory_space=pltpu.VMEM)] * 2,
         out_specs=pl.BlockSpec(memory_space=pltpu.VMEM),
-        name="norm_copies",
+        name="norm_rows",
     )(rows, norm_gain[None])
 
 
-def gather_rows(copies):
-    width = copies.shape[2]
-    rows = swap(copies, PLANE, SQUARES).reshape(-1, width)
-    copies = jnp.broadcast_to(rows[None], (4,) + rows.shape)
-    return swap(copies, PLANE, CROSSES).reshape(-1, width)
+def gather_rows(rows):
+    for groups in (SQUARES, CROSSES):
+        copies = jnp.broadcast_to(rows[None], (4,) + rows.shape)
+        rows = swap(copies, PLANE, groups).reshape(-1, rows.shape[1])
+    return rows
 
 
 def scatter_sum(terms):
-    for groups in (CROSSES, SQUARES):
-        parts = terms.astype(jnp.bfloat16).reshape(4, terms.shape[0] // 4, terms.shape[1])
-        a, b, c, d = [p.astype(jnp.float32) for p in swap(parts, PLANE, groups)]
-        terms = (a + b) + (c + d)
-    return terms
+    chips = SIDE * SIDE
+    parts = terms.astype(jnp.bfloat16).reshape(chips, terms.shape[0] // chips, terms.shape[1])
+    parts = [p.astype(jnp.float32) for p in swap(parts, PLANE, WHOLE)]
+    while len(parts) > 1:
+        parts = [a + b for a, b in zip(parts[::2], parts[1::2])]
+    return parts[0]
 
 
 def row_places(count):
@@ -86,7 +87,8 @@
 
 def earlier_sum(state, reached, lower):
     shape, far, members = state.shape, reached.shape[0], lower.shape[0]
-    cut = swap(state.reshape(members, -1, HD), ("zl", "core"))
+    cut = state.astype(jnp.bfloat16).reshape(members, -1, HD)
+    cut = swap(cut, ("zl", "core")).astype(jnp.float32)
     total = jnp.sum(cut, axis=0).astype(jnp.bfloat16)
     before = jnp.sum(lower * cut[None], axis=1)
     before, total = lax.optimization_barrier((before, total))
@@ -100,11 +102,10 @@
     heads = w_qkv.shape[2] // HD
     reached, lower = earlier_masks()
     place = row_places(tokens.shape[0] * SIDE * SIDE)
-    gains = [head_gain[h * HD : (h + 1) * HD] for h in range(heads)]
-    copies, reached, lower, place, gains = lax.optimization_barrier(
-        (norm_copies(tokens, norm_gain), reached, lower, place, gains)
+    normed, reached, lower, place = lax.optimization_barrier(
+        (norm_rows(tokens, norm_gain), reached, lower, place)
     )
-    gathered = gather_rows(copies)
+    gathered = gather_rows(normed)
     proj = [
         jnp.dot(gathered, w_qkv[:, j], preferred_element_type=jnp.float32).astype(jnp.bfloat16)
         for j in range(3)
@@ -117,7 +118,7 @@
             for k, v in zip(keys, values)
         ]
     )
-    prefix = earlier_sum(state, reached, lower)
+    prefix, gains = lax.optimization_barrier((earlier_sum(state, reached, lower), head_gain))
     causal = place[:, None] >= place[None, :]
     outs = []
     for h in range(heads):
@@ -127,7 +128,7 @@
             query[h], prefix[h], preferred_element_type=jnp.float32
         )
         scale = lax.rsqrt(jnp.mean(attended * attended, axis=-1, keepdims=True) + 1e-05)
-        outs.append((attended * scale * gains[h]).astype(jnp.bfloat16))
+        outs.append((attended * scale * gains[h * HD : (h + 1) * HD]).astype(jnp.bfloat16))
     head_out = jnp.concatenate(outs, axis=1)
     terms = jnp.dot(head_out, w_out, preferred_element_type=jnp.float32)
     return (tokens.astype(jnp.float32) + scatter_sum(terms)).astype(jnp.bfloat16)

time: 144 us -> 144 us (level)
    all_to_all x7 -> x6, blocking collectives: 133 us -> 133 us  [swap(): lax.all_to_all(value, axes, split_axis=0, concat_axis=0, tiled=True, axis...]
where the time goes in v3:
time: 144 us; the launch traced here: 142 us
  blocking collectives  133 us (92%)
  matrix products  4.49 us (3%)
  Pallas kernels  1.85 us (1%)
    all_to_all x6, blocking collectives, swap(): lax.all_to_all(value, axes, split_axis=0, concat_axis=0, tiled=True, axis...  133 us

profile of v3, /device:TPU:24, one launch (start us, length us, event | category | flops | bytes accessed | tf_op | source)
XLA Modules:
  0.0 142.0 jit_solution(13105500112095646303)
XLA Ops:
  0.1 1.8 %norm_rows.1 = bf16[16,4096]{1,0:T(8,128)(2,1)} custom-call(bf16[16,4096]{1,0:T(8,128)(2,1)} %rows_ref.1, f32[1,4096]{1,0:T(1,128)} %bitcast.50), custom_call_target="tpu_custom_call" | custom-call | tf_op jit(solution)/shard_map/norm_rows/pallas_call | solution.py:45
  1.9 0.1 iota.28
  2.0 0.9 broadcast_in_dim.15
  2.9 10.0 %all_to_all.30 = bf16[4,16,4096]{2,1,0:T(8,128)(2,1)S(1)} all-to-all(bf16[4,16,4096]{2,1,0:T(8,128)(2,1)S(1)} %broadcast_in_dim.15), channel_id=1, replica_groups={{0,1,4,5},{2,3,6,7},{8,9,12,13},{10,11,14,15},{21,22,25,26},{23,20,27,2..., dimensions={0} | all-to-all | bytes 1048576 | tf_op jit(solution)/shard_map/all_to_all | solution.py:33
  13.0 0.2 broadcast_in_dim.18
  13.2 33.4 %all_to_all.31 = bf16[4,64,4096]{2,1,0:T(8,128)(2,1)S(1)} all-to-all(bf16[4,64,4096]{2,1,0:T(8,128)(2,1)S(1)} %broadcast_in_dim.18), channel_id=1, replica_groups={{0,3,12,15},{1,2,13,14},{4,7,8,11},{5,6,9,10},{21,20,17,16},{22,23,18,1..., dimensions={0} | all-to-all | bytes 4194304 | tf_op jit(solution)/shard_map/all_to_all | solution.py:33
  46.7 0.7 fusion.17
  47.4 0.7 fusion.14
  48.1 0.7 fusion.11
  48.9 0.0 copy-start.2
  48.9 0.2 fusion.24
  49.1 0.2 fusion.25
  49.3 8.3 %all_to_all.32 = bf16[8,32,128]{2,1,0:T(8,128)(2,1)S(1)} all-to-all(bf16[8,32,128]{2,1,0:T(8,128)(2,1)S(1)} %bitcast.48), channel_id=1, replica_groups=mesh['zh'=8,'zl'=4,'core'=2,'x'=4,'y'=4] {'zl','core'}, dimensions={0} | all-to-all | bytes 131072 | tf_op jit(solution)/shard_map/all_to_all | solution.py:33
  57.6 0.1 multiply_reduce_fusion
  57.7 40.7 %all_to_all.33 = bf16[8,32,128]{2,1,0:T(8,128)(2,1)S(1)} all-to-all(bf16[8,32,128]{2,1,0:T(8,128)(2,1)S(1)} %broadcast_in_dim.20), channel_id=1, replica_groups=mesh['zh'=8,'zl'=4,'core'=2,'x'=4,'y'=4] {'zh'}, dimensions={0} | all-to-all | bytes 131072 | tf_op jit(solution)/shard_map/all_to_all | solution.py:33
  98.5 9.7 %all_to_all.34 = bf16[8,32,128]{2,1,0:T(8,128)(2,1)S(1)} all-to-all(bf16[8,32,128]{2,1,0:T(8,128)(2,1)S(1)} %add_convert_fusion), channel_id=1, replica_groups=mesh['zh'=8,'zl'=4,'core'=2,'x'=4,'y'=4] {'zl','core'}, dimensions={0} | all-to-all | bytes 131072 | tf_op jit(solution)/shard_map/all_to_all | solution.py:33
  108.1 0.2 fusion.38
  108.4 0.2 fusion.52
  108.6 0.4 multiply_reduce_fusion.1
  109.0 0.4 multiply_reduce_fusion.2
  109.4 0.1 multiply_convert_fusion
  109.5 0.7 convolution_convert_fusion
  110.3 30.8 %all_to_all.35 = bf16[16,16,4096]{2,1,0:T(8,128)(2,1)S(1)} all-to-all(bf16[16,16,4096]{2,1,0:T(8,128)(2,1)S(1)} %bitcast.41), channel_id=1, replica_groups={{0,1,4,5,2,3,6,7,8,9,12,13,10,11,14,15},{21,22,25,26,23,20,27,24,29,30,..., dimensions={0} | all-to-all | bytes 4194304 | tf_op jit(solution)/shard_map/all_to_all | solution.py:33
  141.1 0.9 fusion.28
  (18 shorter events, 0.1 us)
Async XLA Ops:
  0.0 109.5 %copy-start = (bf16[256,4096]{1,0:T(8,128)(2,1)S(1)}, bf16[256,4096]{1,0:T(8,128)(2,1)}, u32[]{:S(2)}) copy-start(bf16[256,4096]{1,0:T(8,128)(2,1)} %param.9) | copy-start | bytes 6291460
  13.0 33.7 %copy-start.3 = (bf16[4096,3,256]{2,0,1:T(8,128)(2,1)S(1)}, bf16[4096,3,256]{2,0,1:T(8,128)(2,1)}, u32[]{:S(2)}) copy-start(bf16[4096,3,256]{2,0,1:T(8,128)(2,1)} %param.7) | copy-start | bytes 18874372
  48.9 59.7 %copy-start.2 = (f32[256]{0:T(256)S(1)}, f32[256]{0:T(256)}, u32[]{:S(2)}) copy-start(f32[256]{0:T(256)} %param.8) | copy-start | bytes 3076
  110.2 30.8 %copy-start.1 = (bf16[16,4096]{1,0:T(8,128)(2,1)S(1)}, bf16[16,4096]{1,0:T(8,128)(2,1)}, u32[]{:S(2)}) copy-start(bf16[16,4096]{1,0:T(8,128)(2,1)} %rows_ref.1) | copy-start | bytes 393220

commit v4 on v2

--- a/solution.py
+++ b/solution.py
@@ -1,8 +1,6 @@
 import jax
 import jax.numpy as jnp
 from jax import lax
-from jax.experimental import pallas as pl
-from jax.experimental.pallas import tpu as pltpu
 from jax.sharding import Mesh
 from jax.sharding import PartitionSpec as P
 
@@ -33,29 +31,15 @@
     )
 
 
-def norm_kernel(rows_ref, gain_ref, out_ref):
-    x32 = rows_ref[...].astype(jnp.float32)
+def norm_rows(rows, norm_gain):
+    x32 = rows.astype(jnp.float32)
     scale = lax.rsqrt(jnp.mean(x32 * x32, axis=-1, keepdims=True) + 1e-05)
-    normed = (x32 * scale * gain_ref[...]).astype(jnp.bfloat16)
-    for i in range(out_ref.shape[0]):
-        out_ref[i] = normed
+    return (x32 * scale * norm_gain).astype(jnp.bfloat16)
 
 
-def norm_copies(rows, norm_gain):
-    return pl.pallas_call(
-        norm_kernel,
-        out_shape=jax.ShapeDtypeStruct((4,) + rows.shape, jnp.bfloat16),
-        in_specs=[pl.BlockSpec(memory_space=pltpu.VMEM)] * 2,
-        out_specs=pl.BlockSpec(memory_space=pltpu.VMEM),
-        name="norm_copies",
-    )(rows, norm_gain[None])
-
-
-def gather_rows(copies):
-    width = copies.shape[2]
-    rows = swap(copies, PLANE, SQUARES).reshape(-1, width)
+def spread(rows, groups):
     copies = jnp.broadcast_to(rows[None], (4,) + rows.shape)
-    return swap(copies, PLANE, CROSSES).reshape(-1, width)
+    return swap(copies, PLANE, groups).reshape(-1, rows.shape[1])
 
 
 def scatter_sum(terms):
@@ -86,7 +70,8 @@
 
 def earlier_sum(state, reached, lower):
     shape, far, members = state.shape, reached.shape[0], lower.shape[0]
-    cut = swap(state.reshape(members, -1, HD), ("zl", "core"))
+    cut = state.astype(jnp.bfloat16).reshape(members, -1, HD)
+    cut = swap(cut, ("zl", "core")).astype(jnp.float32)
     total = jnp.sum(cut, axis=0).astype(jnp.bfloat16)
     before = jnp.sum(lower * cut[None], axis=1)
     before, total = lax.optimization_barrier((before, total))
@@ -100,11 +85,9 @@
     heads = w_qkv.shape[2] // HD
     reached, lower = earlier_masks()
     place = row_places(tokens.shape[0] * SIDE * SIDE)
-    gains = [head_gain[h * HD : (h + 1) * HD] for h in range(heads)]
-    copies, reached, lower, place, gains = lax.optimization_barrier(
-        (norm_copies(tokens, norm_gain), reached, lower, place, gains)
-    )
-    gathered = gather_rows(copies)
+    own, reached, lower, place = lax.optimization_barrier((tokens, reached, lower, place))
+    square = spread(own, SQUARES)
+    gathered = spread(norm_rows(square, norm_gain), CROSSES)
     proj = [
         jnp.dot(gathered, w_qkv[:, j], preferred_element_type=jnp.float32).astype(jnp.bfloat16)
         for j in range(3)
@@ -117,7 +100,7 @@
             for k, v in zip(keys, values)
         ]
     )
-    prefix = earlier_sum(state, reached, lower)
+    prefix, gains = lax.optimization_barrier((earlier_sum(state, reached, lower), head_gain))
     causal = place[:, None] >= place[None, :]
     outs = []
     for h in range(heads):
@@ -127,7 +110,7 @@
             query[h], prefix[h], preferred_element_type=jnp.float32
         )
         scale = lax.rsqrt(jnp.mean(attended * attended, axis=-1, keepdims=True) + 1e-05)
-        outs.append((attended * scale * gains[h]).astype(jnp.bfloat16))
+        outs.append((attended * scale * gains[h * HD : (h + 1) * HD]).astype(jnp.bfloat16))
     head_out = jnp.concatenate(outs, axis=1)
     terms = jnp.dot(head_out, w_out, preferred_element_type=jnp.float32)
     return (tokens.astype(jnp.float32) + scatter_sum(terms)).astype(jnp.bfloat16)

time: 144 us -> 142 us (0.986)
  Pallas kernels: 1.86 us -> 0 us
    pallas_call x1 -> x0, Pallas kernels: 1.86 us -> none  [norm_copies(): pl.pallas_call(norm_kernel, out_shape=jax.ShapeDtypeStruct((4,) + rows.sh...]
where the time goes in v4:
time: 142 us; the launch traced here: 140 us
  blocking collectives  132 us (93%)
  matrix products  4.48 us (3%)
  other arithmetic  1.69 us (1%)
  local copies, waits for them, and re-layouts  1.5 us (1%)
    all_to_all x7, blocking collectives, swap(): lax.all_to_all(value, axes, split_axis=0, concat_axis=0, tiled=True, axis...  132 us

profile of v4, /device:TPU:24, one launch (start us, length us, event | category | flops | bytes accessed | tf_op | source)
XLA Modules:
  0.0 139.6 jit_solution(813543556210243359)
XLA Ops:
  0.1 1.1 broadcast_in_dim.10
  1.2 10.0 %all_to_all.35 = bf16[4,16,4096]{2,1,0:T(8,128)(2,1)S(1)} all-to-all(bf16[4,16,4096]{2,1,0:T(8,128)(2,1)S(1)} %broadcast_in_dim.10), channel_id=1, replica_groups={{0,1,4,5},{2,3,6,7},{8,9,12,13},{10,11,14,15},{21,22,25,26},{23,20,27,2..., dimensions={0} | all-to-all | bytes 1048576 | tf_op jit(solution)/shard_map/all_to_all | solution.py:29
  11.2 0.2 multiply_reduce_fusion.1
  11.5 0.2 fusion.27
  11.7 0.2 broadcast_in_dim.11
  12.0 33.3 %all_to_all.36 = bf16[4,64,4096]{2,1,0:T(8,128)(2,1)S(1)} all-to-all(bf16[4,64,4096]{2,1,0:T(8,128)(2,1)S(1)} %broadcast_in_dim.11), channel_id=1, replica_groups={{0,3,12,15},{1,2,13,14},{4,7,8,11},{5,6,9,10},{21,20,17,16},{22,23,18,1..., dimensions={0} | all-to-all | bytes 4194304 | tf_op jit(solution)/shard_map/all_to_all | solution.py:29
  45.3 0.7 fusion.17
  46.0 0.7 fusion.14
  46.8 0.7 fusion.11
  47.5 0.2 fusion.24
  47.7 0.2 fusion.25
  47.9 8.3 %all_to_all.37 = bf16[8,32,128]{2,1,0:T(8,128)(2,1)S(1)} all-to-all(bf16[8,32,128]{2,1,0:T(8,128)(2,1)S(1)} %bitcast.53), channel_id=1, replica_groups=mesh['zh'=8,'zl'=4,'core'=2,'x'=4,'y'=4] {'zl','core'}, dimensions={0} | all-to-all | bytes 131072 | tf_op jit(solution)/shard_map/all_to_all | solution.py:29
  56.3 40.9 %all_to_all.38 = bf16[8,32,128]{2,1,0:T(8,128)(2,1)S(1)} all-to-all(bf16[8,32,128]{2,1,0:T(8,128)(2,1)S(1)} %broadcast_in_dim.13), channel_id=1, replica_groups=mesh['zh'=8,'zl'=4,'core'=2,'x'=4,'y'=4] {'zh'}, dimensions={0} | all-to-all | bytes 131072 | tf_op jit(solution)/shard_map/all_to_all | solution.py:29
  97.3 9.7 %all_to_all.39 = bf16[8,32,128]{2,1,0:T(8,128)(2,1)S(1)} all-to-all(bf16[8,32,128]{2,1,0:T(8,128)(2,1)S(1)} %add_convert_fusion.1), channel_id=1, replica_groups=mesh['zh'=8,'zl'=4,'core'=2,'x'=4,'y'=4] {'zl','core'}, dimensions={0} | all-to-all | bytes 131072 | tf_op jit(solution)/shard_map/all_to_all | solution.py:29
  106.9 0.2 fusion.40
  107.1 0.2 fusion.54
  107.4 0.4 multiply_reduce_fusion.2
  107.8 0.4 multiply_reduce_fusion.3
  108.2 0.1 multiply_convert_fusion
  108.3 0.7 convolution_convert_fusion
  109.0 20.4 %all_to_all.40 = bf16[4,64,4096]{2,1,0:T(8,128)(2,1)S(1)} all-to-all(bf16[4,64,4096]{2,1,0:T(8,128)(2,1)S(1)} %bitcast.46), channel_id=1, replica_groups={{0,3,12,15},{1,2,13,14},{4,7,8,11},{5,6,9,10},{21,20,17,16},{22,23,18,1..., dimensions={0} | all-to-all | bytes 4194304 | tf_op jit(solution)/shard_map/all_to_all | solution.py:29
  129.5 0.3 add_convert_fusion
  129.7 9.1 %all_to_all.41 = bf16[4,16,4096]{2,1,0:T(8,128)(2,1)S(1)} all-to-all(bf16[4,16,4096]{2,1,0:T(8,128)(2,1)S(1)} %bitcast.47), channel_id=1, replica_groups={{0,1,4,5},{2,3,6,7},{8,9,12,13},{10,11,14,15},{21,22,25,26},{23,20,27,2..., dimensions={0} | all-to-all | bytes 1048576 | tf_op jit(solution)/shard_map/all_to_all | solution.py:29
  138.9 0.7 fusion.30
  (25 shorter events, 0.4 us)
Async XLA Ops:
  0.0 108.3 %copy-start = (bf16[256,4096]{1,0:T(8,128)(2,1)S(1)}, bf16[256,4096]{1,0:T(8,128)(2,1)}, u32[]{:S(2)}) copy-start(bf16[256,4096]{1,0:T(8,128)(2,1)} %param.9) | copy-start | bytes 6291460
  0.0 11.5 %copy-start.2 = (f32[4096]{0:T(1024)S(1)}, f32[4096]{0:T(1024)}, u32[]{:S(2)}) copy-start(f32[4096]{0:T(1024)} %param.6) | copy-start | bytes 49156
  11.7 33.6 %copy-start.4 = (bf16[4096,3,256]{2,0,1:T(8,128)(2,1)S(1)}, bf16[4096,3,256]{2,0,1:T(8,128)(2,1)}, u32[]{:S(2)}) copy-start(bf16[4096,3,256]{2,0,1:T(8,128)(2,1)} %param.7) | copy-start | bytes 18874372
  47.5 59.9 %copy-start.3 = (f32[256]{0:T(256)S(1)}, f32[256]{0:T(256)}, u32[]{:S(2)}) copy-start(f32[256]{0:T(256)} %param.8) | copy-start | bytes 3076
  129.5 9.4 %copy-start.1 = (bf16[16,4096]{1,0:T(8,128)(2,1)S(1)}, bf16[16,4096]{1,0:T(8,128)(2,1)}, u32[]{:S(2)}) copy-start(bf16[16,4096]{1,0:T(8,128)(2,1)} %param.5) | copy-start | bytes 393220

commit v5 on v4

--- a/solution.py
+++ b/solution.py
@@ -3,6 +3,7 @@
 from jax import lax
 from jax.sharding import Mesh
 from jax.sharding import PartitionSpec as P
+
 
 HD = 128
 SIDE = 4
@@ -25,6 +26,28 @@
 ]
 
 
+FLIPS = BITS[1:]
+FETCHED = 2
+
+
+def fetch(value, ax, ay):
+    pairs = []
+    for c in range(2):
+        for jx, jy in BITS:
+            for bx, by in BITS:
+                tx, ty = bx ^ ax, by ^ ay
+                source = spot(c, bx, by, (bx + jx) % 2, (by + jy) % 2)
+                pairs.append((source, spot(c, tx, ty, (tx + jx) % 2, (ty + jy) % 2)))
+    return lax.ppermute(value, PLANE, pairs)
+
+
+def partner_slots():
+    core = lax.axis_index("core")
+    bx = ((lax.axis_index("x") - core) & (SIDE - 1)) >> 1
+    by = ((lax.axis_index("y") - core) & (SIDE - 1)) >> 1
+    return [((2 * bx + by) ^ k).astype(jnp.uint32) for k in range(4)]
+
+
 def swap(value, axes, groups=None):
     return lax.all_to_all(
         value, axes, split_axis=0, concat_axis=0, tiled=True, axis_index_groups=groups
@@ -42,12 +65,29 @@
     return swap(copies, PLANE, groups).reshape(-1, rows.shape[1])
 
 
-def scatter_sum(terms):
-    for groups in (CROSSES, SQUARES):
-        parts = terms.astype(jnp.bfloat16).reshape(4, terms.shape[0] // 4, terms.shape[1])
-        a, b, c, d = [p.astype(jnp.float32) for p in swap(parts, PLANE, groups)]
-        terms = (a + b) + (c + d)
-    return terms
+def stage_parts(terms):
+    return terms.reshape(4, terms.shape[0] // 4, terms.shape[1])
+
+
+def add_parts(parts):
+    a, b, c, d = [p.astype(jnp.float32) for p in parts]
+    return (a + b) + (c + d)
+
+
+def project_sum(head_out, w_out, fetched, slots):
+    width = fetched[0].shape[1]
+    terms = jnp.dot(head_out, w_out[:, width:], preferred_element_type=jnp.float32)
+    rest = terms.shape[1]
+    mixed = jnp.concatenate([terms.astype(jnp.bfloat16), head_out], axis=1)
+    mixed = swap(stage_parts(mixed), PLANE, CROSSES)
+    later = add_parts(mixed[:, :, :rest])
+    heads = mixed[:, :, rest:]
+    first = 0.0
+    for slot, w in zip(slots, fetched):
+        rows = lax.dynamic_index_in_dim(heads, slot, 0, keepdims=False)
+        first = first + jnp.dot(rows, w, preferred_element_type=jnp.float32)
+    terms = jnp.concatenate([first, later], axis=1).astype(jnp.bfloat16)
+    return add_parts(swap(stage_parts(terms), PLANE, SQUARES))
 
 
 def row_places(count):
@@ -81,11 +121,15 @@
     return swap(prefix, ("zl", "core")).reshape(shape)
 
 
-def local(tokens, norm_gain, w_qkv, head_gain, w_out):
+def layer(tokens, norm_gain, w_qkv, head_gain, w_out):
     heads = w_qkv.shape[2] // HD
     reached, lower = earlier_masks()
     place = row_places(tokens.shape[0] * SIDE * SIDE)
-    own, reached, lower, place = lax.optimization_barrier((tokens, reached, lower, place))
+    columns = w_out[:, : w_out.shape[1] // FETCHED]
+    own, reached, lower, place, slots = lax.optimization_barrier(
+        (tokens, reached, lower, place, partner_slots())
+    )
+    fetched = [columns] + [fetch(columns, ax, ay) for ax, ay in FLIPS]
     square = spread(own, SQUARES)
     gathered = spread(norm_rows(square, norm_gain), CROSSES)
     proj = [
@@ -112,15 +156,15 @@
         scale = lax.rsqrt(jnp.mean(attended * attended, axis=-1, keepdims=True) + 1e-05)
         outs.append((attended * scale * gains[h * HD : (h + 1) * HD]).astype(jnp.bfloat16))
     head_out = jnp.concatenate(outs, axis=1)
-    terms = jnp.dot(head_out, w_out, preferred_element_type=jnp.float32)
-    return (tokens.astype(jnp.float32) + scatter_sum(terms)).astype(jnp.bfloat16)
+    summed = project_sum(head_out, w_out, fetched, slots)
+    return (tokens.astype(jnp.float32) + summed).astype(jnp.bfloat16)
 
 
 def solution(mesh):
     context = mesh.shape["context"]
     cut = Mesh(mesh.devices.reshape(context // (2 * NEAR), NEAR, 2, SIDE, SIDE), ALL)
     return jax.shard_map(
-        local,
+        layer,
         mesh=cut,
         in_specs=(
             P(ALL, None),

time: 142 us -> 165 us (1.16)
  blocking collectives: 132 us -> 111 us
  waiting for transfers between devices: 0 us -> 18.8 us
  starting transfers between devices: 0 us -> 17.4 us
  matrix products: 4.48 us -> 9.11 us
    all_to_all x7 -> x6, blocking collectives: 132 us -> 111 us  [swap(): lax.all_to_all(value, axes, split_axis=0, concat_axis=0, tiled=True, axis...]
    ppermute x0 -> x3, waiting for transfers between devices: none -> 18.8 us  [fetch(): return lax.ppermute(value, PLANE, pairs)]
    ppermute x0 -> x3, starting transfers between devices: none -> 11.6 us  [fetch(): return lax.ppermute(value, PLANE, pairs)]
    all_to_all x0 -> x1, starting transfers between devices: none -> 5.81 us  [swap(): lax.all_to_all(value, axes, split_axis=0, concat_axis=0, tiled=True, axis...]
    dot_general x10 -> x14, matrix products: 4.48 us -> 9.11 us  [the longest x4 4.91 us: project_sum(): first = first + jnp.dot(rows, w, preferred_element_type=jnp.float32)]
  transfers between devices with their start and end apart: 0 -> 4, of which waited for: 0 -> 2; matrix products, arithmetic and copies ran while one was open for 0% -> 3% of each run, Pallas kernels for 0% -> 0%
where the time goes in v5:
time: 165 us; the launch traced here: 162 us
  blocking collectives  111 us (67%)
  waiting for transfers between devices  18.8 us (11%)
  starting transfers between devices  17.4 us (11%)
  matrix products  9.11 us (6%)
  local copies, waits for them, and re-layouts  2.72 us (2%)
  other arithmetic  2.7 us (2%)
    all_to_all x6, blocking collectives, swap(): lax.all_to_all(value, axes, split_axis=0, concat_axis=0, tiled=True, axis...  111 us
    ppermute x3, waiting for transfers between devices, fetch(): return lax.ppermute(value, PLANE, pairs)  18.8 us
    ppermute x3, starting transfers between devices, fetch(): return lax.ppermute(value, PLANE, pairs)  11.6 us
    all_to_all x1, starting transfers between devices, swap(): lax.all_to_all(value, axes, split_axis=0, concat_axis=0, tiled=True, axis...  5.81 us
    dot_general x4, matrix products, project_sum(): first = first + jnp.dot(rows, w, preferred_element_type=jnp.float32)  4.91 us
  transfers between devices with their start and end apart: 4, of which 2 were waited for; matrix products, arithmetic and copies ran while one was open for 3% of the time, Pallas kernels for 0%

profile of v5, /device:TPU:24, one launch (start us, length us, event | category | flops | bytes accessed | tf_op | source)
XLA Modules:
  0.0 162.5 jit_solution(14274895972867681173)
XLA Ops:
  0.1 0.9 broadcast_in_dim.10
  1.1 10.0 %all_to_all.35 = bf16[4,16,4096]{2,1,0:T(8,128)(2,1)S(1)} all-to-all(bf16[4,16,4096]{2,1,0:T(8,128)(2,1)S(1)} %broadcast_in_dim.10), channel_id=1, replica_groups={{0,1,4,5},{2,3,6,7},{8,9,12,13},{10,11,14,15},{21,22,25,26},{23,20,27,2..., dimensions={0} | all-to-all | bytes 1048576 | tf_op jit(solution)/shard_map/all_to_all | solution.py:52
  11.9 33.3 %all_to_all.36 = bf16[4,64,4096]{2,1,0:T(8,128)(2,1)S(1)} all-to-all(bf16[4,64,4096]{2,1,0:T(8,128)(2,1)S(1)} %broadcast_in_dim.11), channel_id=1, replica_groups={{0,3,12,15},{1,2,13,14},{4,7,8,11},{5,6,9,10},{21,20,17,16},{22,23,18,1..., dimensions={0} | all-to-all | bytes 4194304 | tf_op jit(solution)/shard_map/all_to_all | solution.py:52
  45.2 0.7 fusion.13
  45.9 0.7 fusion.16
  46.6 0.7 fusion.19
  47.8 8.4 %all_to_all.37 = bf16[8,32,128]{2,1,0:T(8,128)(2,1)S(1)} all-to-all(bf16[8,32,128]{2,1,0:T(8,128)(2,1)S(1)} %bitcast.68), channel_id=1, replica_groups=mesh['zh'=8,'zl'=4,'core'=2,'x'=4,'y'=4] {'zl','core'}, dimensions={0} | all-to-all | bytes 131072 | tf_op jit(solution)/shard_map/all_to_all | solution.py:52
  56.4 40.9 %all_to_all.38 = bf16[8,32,128]{2,1,0:T(8,128)(2,1)S(1)} all-to-all(bf16[8,32,128]{2,1,0:T(8,128)(2,1)S(1)} %broadcast_in_dim.13), channel_id=1, replica_groups=mesh['zh'=8,'zl'=4,'core'=2,'x'=4,'y'=4] {'zh'}, dimensions={0} | all-to-all | bytes 131072 | tf_op jit(solution)/shard_map/all_to_all | solution.py:52
  97.3 9.7 %all_to_all.39 = bf16[8,32,128]{2,1,0:T(8,128)(2,1)S(1)} all-to-all(bf16[8,32,128]{2,1,0:T(8,128)(2,1)S(1)} %add_convert_fusion.1), channel_id=1, replica_groups=mesh['zh'=8,'zl'=4,'core'=2,'x'=4,'y'=4] {'zl','core'}, dimensions={0} | all-to-all | bytes 131072 | tf_op jit(solution)/shard_map/all_to_all | solution.py:52
  107.4 0.4 multiply_reduce_fusion.2
  108.6 0.5 convolution_convert_fusion
  109.0 1.1 pad_maximum_fusion
  110.1 5.8 %all-to-all-start.5 = ((bf16[4,64,2304]{2,1,0:T(8,128)(2,1)}), bf16[4,64,2304]{2,1,0:T(8,128)(2,1)S(1)}, u32[]{:S(2)}, u32[]{:S(2)}) async-start(bf16[4,64,2304]{2,1,0:T(8,128)(2,1)} %bitcast.13), calls=%async_computation.5 | async-start | bytes 2359296 | tf_op jit(solution)/shard_map/all_to_all | solution.py:52
  115.9 1.1 slice.68
  117.0 4.6 %collective-permute-start.2 = (bf16[256,2048]{1,0:T(8,128)(2,1)}, bf16[256,2048]{1,0:T(8,128)(2,1)}, u32[]{:S(2)}, u32[]{:S(2)}) collective-permute-start(bf16[256,2048]{1,0:T(8,128)(2,1)} %slice.68), channel_id=1, source_target_pairs={{0,15},{3,12},{12,3},{15,0},{1,14},{2,13},{13,2},{14,1},{4,11},{7,... | collective-permute-start | bytes 3145736 | tf_op jit(solution)/shard_map/ppermute | solution.py:41
  121.6 4.6 %collective-permute-start = (bf16[256,2048]{1,0:T(8,128)(2,1)}, bf16[256,2048]{1,0:T(8,128)(2,1)}, u32[]{:S(2)}, u32[]{:S(2)}) collective-permute-start(bf16[256,2048]{1,0:T(8,128)(2,1)} %slice.68), channel_id=1, source_target_pairs={{0,3},{3,0},{12,15},{15,12},{1,2},{2,1},{13,14},{14,13},{4,7},{7,4... | collective-permute-start | bytes 3145736 | tf_op jit(solution)/shard_map/ppermute | solution.py:41
  126.2 2.5 %collective-permute-start.1 = (bf16[256,2048]{1,0:T(8,128)(2,1)}, bf16[256,2048]{1,0:T(8,128)(2,1)}, u32[]{:S(2)}, u32[]{:S(2)}) collective-permute-start(bf16[256,2048]{1,0:T(8,128)(2,1)} %slice.68), channel_id=1, source_target_pairs={{0,12},{3,15},{12,0},{15,3},{1,13},{2,14},{13,1},{14,2},{4,8},{7,1... | collective-permute-start | bytes 3145736 | tf_op jit(solution)/shard_map/ppermute | solution.py:41
  129.0 9.1 %collective-permute-done.2 = bf16[256,2048]{1,0:T(8,128)(2,1)} collective-permute-done((bf16[256,2048]{1,0:T(8,128)(2,1)}, bf16[256,2048]{1,0:T(8,128)(2,1)}, u32[]{:S(2)}, u32[]{:S(2)}) %collective-permute-start.2) | collective-permute-done | bytes 1048608 | tf_op jit(solution)/shard_map/ppermute | solution.py:41
  138.2 1.5 fusion.61
  139.7 9.6 %collective-permute-done = bf16[256,2048]{1,0:T(8,128)(2,1)} collective-permute-done((bf16[256,2048]{1,0:T(8,128)(2,1)}, bf16[256,2048]{1,0:T(8,128)(2,1)}, u32[]{:S(2)}, u32[]{:S(2)}) %collective-permute-start) | collective-permute-done | bytes 1048608 | tf_op jit(solution)/shard_map/ppermute | solution.py:41
  149.3 1.5 convolution_add_fusion.1
  151.0 1.6 fusion.1
  152.6 9.1 %all_to_all.40 = bf16[4,16,4096]{2,1,0:T(8,128)(2,1)S(1)} all-to-all(bf16[4,16,4096]{2,1,0:T(8,128)(2,1)S(1)} %pad_maximum_fusion.1), channel_id=1, replica_groups={{0,1,4,5},{2,3,6,7},{8,9,12,13},{10,11,14,15},{21,22,25,26},{23,20,27,2..., dimensions={0} | all-to-all | bytes 1048576 | tf_op jit(solution)/shard_map/all_to_all | solution.py:52
  161.7 0.7 fusion.33
  (42 shorter events, 3.0 us)
Async XLA Ops:
  0.0 11.4 %copy-start.2 = (f32[4096]{0:T(1024)S(1)}, f32[4096]{0:T(1024)}, u32[]{:S(2)}) copy-start(f32[4096]{0:T(1024)} %param.6) | copy-start | bytes 49156
  11.6 33.6 %copy-start.4 = (bf16[4096,3,256]{2,0,1:T(8,128)(2,1)S(1)}, bf16[4096,3,256]{2,0,1:T(8,128)(2,1)}, u32[]{:S(2)}) copy-start(bf16[4096,3,256]{2,0,1:T(8,128)(2,1)} %param.7) | copy-start | bytes 18874372
  47.4 60.0 %copy-start.3 = (f32[256]{0:T(256)S(1)}, f32[256]{0:T(256)}, u32[]{:S(2)}) copy-start(f32[256]{0:T(256)} %param.8) | copy-start | bytes 3076
  47.4 61.2 %copy-start = (bf16[256,4096]{1,0:T(8,128)(2,1)S(1)}, bf16[256,4096]{1,0:T(8,128)(2,1)}, u32[]{:S(2)}) copy-start(bf16[256,4096]{1,0:T(8,128)(2,1)} %param.9) | copy-start | bytes 6291460
  110.1 18.6 %all-to-all-start.5 = ((bf16[4,64,2304]{2,1,0:T(8,128)(2,1)}), bf16[4,64,2304]{2,1,0:T(8,128)(2,1)S(1)}, u32[]{:S(2)}, u32[]{:S(2)}) async-start(bf16[4,64,2304]{2,1,0:T(8,128)(2,1)} %bitcast.13), calls=%async_computation.5 | async-start | bytes 2359296 | tf_op jit(solution)/shard_map/all_to_all | solution.py:52
  117.0 21.1 %collective-permute-start.2 = (bf16[256,2048]{1,0:T(8,128)(2,1)}, bf16[256,2048]{1,0:T(8,128)(2,1)}, u32[]{:S(2)}, u32[]{:S(2)}) collective-permute-start(bf16[256,2048]{1,0:T(8,128)(2,1)} %slice.68), channel_id=1, source_target_pairs={{0,15},{3,12},{12,3},{15,0},{1,14},{2,13},{13,2},{14,1},{4,11},{7,... | collective-permute-start | bytes 3145736 | tf_op jit(solution)/shard_map/ppermute | solution.py:41
  121.6 27.7 %collective-permute-start = (bf16[256,2048]{1,0:T(8,128)(2,1)}, bf16[256,2048]{1,0:T(8,128)(2,1)}, u32[]{:S(2)}, u32[]{:S(2)}) collective-permute-start(bf16[256,2048]{1,0:T(8,128)(2,1)} %slice.68), channel_id=1, source_target_pairs={{0,3},{3,0},{12,15},{15,12},{1,2},{2,1},{13,14},{14,13},{4,7},{7,4... | collective-permute-start | bytes 3145736 | tf_op jit(solution)/shard_map/ppermute | solution.py:41
  126.2 24.8 %collective-permute-start.1 = (bf16[256,2048]{1,0:T(8,128)(2,1)}, bf16[256,2048]{1,0:T(8,128)(2,1)}, u32[]{:S(2)}, u32[]{:S(2)}) collective-permute-start(bf16[256,2048]{1,0:T(8,128)(2,1)} %slice.68), channel_id=1, source_target_pairs={{0,12},{3,15},{12,0},{15,3},{1,13},{2,14},{13,1},{14,2},{4,8},{7,1... | collective-permute-start | bytes 3145736 | tf_op jit(solution)/shard_map/ppermute | solution.py:41
  151.0 10.8 %copy-start.1 = (bf16[16,4096]{1,0:T(8,128)(2,1)S(1)}, bf16[16,4096]{1,0:T(8,128)(2,1)}, u32[]{:S(2)}) copy-start(bf16[16,4096]{1,0:T(8,128)(2,1)} %param.5) | copy-start | bytes 393220

commit v6 on v4

--- a/solution.py
+++ b/solution.py
@@ -12,7 +12,7 @@
 
 
 def spot(core, bx, by, px, py):
-    x, y = (core + 2 * bx + px) % SIDE, (core + 2 * by + py) % SIDE
+    x, y = (core + 2 * bx + px) % SIDE, (1 - core + 2 * by + py) % SIDE
     return core * SIDE * SIDE + x * SIDE + y
 
 
@@ -56,7 +56,7 @@
     core = lax.axis_index("core")
     slot = i // part
     bx, by, px, py = slot // 8, slot // 4 % 2, slot // 2 % 2, slot % 2
-    x, y = (core + 2 * bx + px) % SIDE, (core + 2 * by + py) % SIDE
+    x, y = (core + 2 * bx + px) % SIDE, (1 - core + 2 * by + py) % SIDE
     return (x * SIDE + y) * part + i % part
 
 

time: 142 us -> 141 us (level); the launches traced: 140 us -> 140 us
  no operation moved by 1% of the time
where the time goes in v6:
time: 141 us; the launch traced here: 140 us
  blocking collectives  132 us (94%)
  matrix products  4.48 us (3%)
  other arithmetic  1.69 us (1%)
  local copies, waits for them, and re-layouts  1.5 us (1%)
    all_to_all x7, blocking collectives, swap(): lax.all_to_all(value, axes, split_axis=0, concat_axis=0, tiled=True, axis...  132 us

profile of v6, /device:TPU:24, one launch (start us, length us, event | category | flops | bytes accessed | tf_op | source)
XLA Modules:
  0.0 140.1 jit_solution(1511014787268357788)
XLA Ops:
  0.1 1.1 broadcast_in_dim.10
  1.2 24.9 %all_to_all.35 = bf16[4,16,4096]{2,1,0:T(8,128)(2,1)S(1)} all-to-all(bf16[4,16,4096]{2,1,0:T(8,128)(2,1)S(1)} %broadcast_in_dim.10), channel_id=1, replica_groups={{1,2,5,6},{3,0,7,4},{9,10,13,14},{11,8,15,12},{20,21,24,25},{22,23,26,2..., dimensions={0} | all-to-all | bytes 1048576 | tf_op jit(solution)/shard_map/all_to_all | solution.py:29
  26.1 0.2 multiply_reduce_fusion.1
  26.3 0.2 fusion.27
  26.6 0.2 broadcast_in_dim.11
  26.8 19.0 %all_to_all.36 = bf16[4,64,4096]{2,1,0:T(8,128)(2,1)S(1)} all-to-all(bf16[4,64,4096]{2,1,0:T(8,128)(2,1)S(1)} %broadcast_in_dim.11), channel_id=1, replica_groups={{1,0,13,12},{2,3,14,15},{5,4,9,8},{6,7,10,11},{20,23,16,19},{21,22,17,1..., dimensions={0} | all-to-all | bytes 4194304 | tf_op jit(solution)/shard_map/all_to_all | solution.py:29
  45.8 0.7 fusion.17
  46.6 0.7 fusion.14
  47.3 0.7 fusion.11
  48.0 0.2 fusion.24
  48.2 0.2 fusion.25
  48.5 8.3 %all_to_all.37 = bf16[8,32,128]{2,1,0:T(8,128)(2,1)S(1)} all-to-all(bf16[8,32,128]{2,1,0:T(8,128)(2,1)S(1)} %bitcast.53), channel_id=1, replica_groups=mesh['zh'=8,'zl'=4,'core'=2,'x'=4,'y'=4] {'zl','core'}, dimensions={0} | all-to-all | bytes 131072 | tf_op jit(solution)/shard_map/all_to_all | solution.py:29
  56.9 40.5 %all_to_all.38 = bf16[8,32,128]{2,1,0:T(8,128)(2,1)S(1)} all-to-all(bf16[8,32,128]{2,1,0:T(8,128)(2,1)S(1)} %broadcast_in_dim.13), channel_id=1, replica_groups=mesh['zh'=8,'zl'=4,'core'=2,'x'=4,'y'=4] {'zh'}, dimensions={0} | all-to-all | bytes 131072 | tf_op jit(solution)/shard_map/all_to_all | solution.py:29
  97.4 9.7 %all_to_all.39 = bf16[8,32,128]{2,1,0:T(8,128)(2,1)S(1)} all-to-all(bf16[8,32,128]{2,1,0:T(8,128)(2,1)S(1)} %add_convert_fusion.1), channel_id=1, replica_groups=mesh['zh'=8,'zl'=4,'core'=2,'x'=4,'y'=4] {'zl','core'}, dimensions={0} | all-to-all | bytes 131072 | tf_op jit(solution)/shard_map/all_to_all | solution.py:29
  107.1 0.2 fusion.40
  107.3 0.2 fusion.54
  107.5 0.4 multiply_reduce_fusion.2
  107.9 0.4 multiply_reduce_fusion.3
  108.3 0.1 multiply_convert_fusion
  108.4 0.7 convolution_convert_fusion
  109.2 19.2 %all_to_all.40 = bf16[4,64,4096]{2,1,0:T(8,128)(2,1)S(1)} all-to-all(bf16[4,64,4096]{2,1,0:T(8,128)(2,1)S(1)} %bitcast.46), channel_id=1, replica_groups={{1,0,13,12},{2,3,14,15},{5,4,9,8},{6,7,10,11},{20,23,16,19},{21,22,17,1..., dimensions={0} | all-to-all | bytes 4194304 | tf_op jit(solution)/shard_map/all_to_all | solution.py:29
  128.4 0.3 add_convert_fusion
  128.7 10.7 %all_to_all.41 = bf16[4,16,4096]{2,1,0:T(8,128)(2,1)S(1)} all-to-all(bf16[4,16,4096]{2,1,0:T(8,128)(2,1)S(1)} %bitcast.47), channel_id=1, replica_groups={{1,2,5,6},{3,0,7,4},{9,10,13,14},{11,8,15,12},{20,21,24,25},{22,23,26,2..., dimensions={0} | all-to-all | bytes 1048576 | tf_op jit(solution)/shard_map/all_to_all | solution.py:29
  139.4 0.7 fusion.30
  (25 shorter events, 0.4 us)
Async XLA Ops:
  0.0 108.4 %copy-start = (bf16[256,4096]{1,0:T(8,128)(2,1)S(1)}, bf16[256,4096]{1,0:T(8,128)(2,1)}, u32[]{:S(2)}) copy-start(bf16[256,4096]{1,0:T(8,128)(2,1)} %param.9) | copy-start | bytes 6291460
  0.0 26.3 %copy-start.2 = (f32[4096]{0:T(1024)S(1)}, f32[4096]{0:T(1024)}, u32[]{:S(2)}) copy-start(f32[4096]{0:T(1024)} %param.6) | copy-start | bytes 49156
  26.6 19.3 %copy-start.4 = (bf16[4096,3,256]{2,0,1:T(8,128)(2,1)S(1)}, bf16[4096,3,256]{2,0,1:T(8,128)(2,1)}, u32[]{:S(2)}) copy-start(bf16[4096,3,256]{2,0,1:T(8,128)(2,1)} %param.7) | copy-start | bytes 18874372
  48.0 59.5 %copy-start.3 = (f32[256]{0:T(256)S(1)}, f32[256]{0:T(256)}, u32[]{:S(2)}) copy-start(f32[256]{0:T(256)} %param.8) | copy-start | bytes 3076
  128.4 11.0 %copy-start.1 = (bf16[16,4096]{1,0:T(8,128)(2,1)S(1)}, bf16[16,4096]{1,0:T(8,128)(2,1)}, u32[]{:S(2)}) copy-start(bf16[16,4096]{1,0:T(8,128)(2,1)} %param.5) | copy-start | bytes 393220

commit v7 on v5

--- a/solution.py
+++ b/solution.py
@@ -1,6 +1,8 @@
 import jax
 import jax.numpy as jnp
 from jax import lax
+from jax.experimental import pallas as pl
+from jax.experimental.pallas import tpu as pltpu
 from jax.sharding import Mesh
 from jax.sharding import PartitionSpec as P
 
@@ -13,7 +15,7 @@
 
 
 def spot(core, bx, by, px, py):
-    x, y = (core + 2 * bx + px) % SIDE, (core + 2 * by + py) % SIDE
+    x, y = (core + 2 * bx + px) % SIDE, (1 - core + 2 * by + py) % SIDE
     return core * SIDE * SIDE + x * SIDE + y
 
 
@@ -44,8 +46,8 @@
 def partner_slots():
     core = lax.axis_index("core")
     bx = ((lax.axis_index("x") - core) & (SIDE - 1)) >> 1
-    by = ((lax.axis_index("y") - core) & (SIDE - 1)) >> 1
-    return [((2 * bx + by) ^ k).astype(jnp.uint32) for k in range(4)]
+    by = ((lax.axis_index("y") - 1 + core) & (SIDE - 1)) >> 1
+    return jnp.stack([(2 * bx + by) ^ k for k in range(4)])
 
 
 def swap(value, axes, groups=None):
@@ -72,6 +74,32 @@
 def add_parts(parts):
     a, b, c, d = [p.astype(jnp.float32) for p in parts]
     return (a + b) + (c + d)
+
+
+def products_kernel(slots_ref, heads_ref, *refs):
+    total = 0.0
+    for k, w_ref in enumerate(refs[:-1]):
+        rows = heads_ref[slots_ref[k]]
+        total += jnp.dot(rows, w_ref[...], preferred_element_type=jnp.float32)
+    refs[-1][...] = total.astype(jnp.bfloat16)
+
+
+def products(heads, slots, fetched):
+    depth, width = fetched[0].shape
+    tile = 512
+    held = pl.BlockSpec(heads.shape, lambda i, s: (0, 0, 0))
+    block = pl.BlockSpec((depth, tile), lambda i, s: (0, i))
+    return pl.pallas_call(
+        products_kernel,
+        out_shape=jax.ShapeDtypeStruct((heads.shape[1], width), jnp.bfloat16),
+        grid_spec=pltpu.PrefetchScalarGridSpec(
+            num_scalar_prefetch=1,
+            grid=(width // tile,),
+            in_specs=[held] + [block] * 4,
+            out_specs=pl.BlockSpec((heads.shape[1], tile), lambda i, s: (0, i)),
+        ),
+        name="products",
+    )(slots, heads, *fetched)
 
 
 def project_sum(head_out, w_out, fetched, slots):
@@ -79,14 +107,13 @@
     terms = jnp.dot(head_out, w_out[:, width:], preferred_element_type=jnp.float32)
     rest = terms.shape[1]
     mixed = jnp.concatenate([terms.astype(jnp.bfloat16), head_out], axis=1)
+    mixed, fetched = lax.optimization_barrier((mixed, fetched))
     mixed = swap(stage_parts(mixed), PLANE, CROSSES)
     later = add_parts(mixed[:, :, :rest])
     heads = mixed[:, :, rest:]
-    first = 0.0
-    for slot, w in zip(slots, fetched):
-        rows = lax.dynamic_index_in_dim(heads, slot, 0, keepdims=False)
-        first = first + jnp.dot(rows, w, preferred_element_type=jnp.float32)
-    terms = jnp.concatenate([first, later], axis=1).astype(jnp.bfloat16)
+    first = products(heads, slots, fetched)
+    later = later.astype(jnp.bfloat16)
+    terms = jnp.concatenate([first, later], axis=1)
     return add_parts(swap(stage_parts(terms), PLANE, SQUARES))
 
 
@@ -96,7 +123,7 @@
     core = lax.axis_index("core")
     slot = i // part
     bx, by, px, py = slot // 8, slot // 4 % 2, slot // 2 % 2, slot % 2
-    x, y = (core + 2 * bx + px) % SIDE, (core + 2 * by + py) % SIDE
+    x, y = (core + 2 * bx + px) % SIDE, (1 - core + 2 * by + py) % SIDE
     return (x * SIDE + y) * part + i % part
 
 
@@ -108,28 +135,29 @@
     return (group < lax.axis_index("zh")).astype(jnp.float32), (since < to).astype(jnp.float32)
 
 
-def earlier_sum(state, reached, lower):
+def earlier_sum(state, reached, lower, intra, w_out):
     shape, far, members = state.shape, reached.shape[0], lower.shape[0]
     cut = state.astype(jnp.bfloat16).reshape(members, -1, HD)
     cut = swap(cut, ("zl", "core")).astype(jnp.float32)
     total = jnp.sum(cut, axis=0).astype(jnp.bfloat16)
     before = jnp.sum(lower * cut[None], axis=1)
-    before, total = lax.optimization_barrier((before, total))
+    before, total, w_out = lax.optimization_barrier((before, total, w_out))
+    columns = w_out[:, : w_out.shape[1] // FETCHED]
+    fetched = [columns] + [fetch(columns, ax, ay) for ax, ay in FLIPS]
     totals = swap(jnp.broadcast_to(total[None], (far,) + total.shape), ("zh",))
     base = jnp.sum(reached * totals.astype(jnp.float32), axis=0)
     prefix = (before + base).astype(jnp.bfloat16)
-    return swap(prefix, ("zl", "core")).reshape(shape)
+    prefix, intra = lax.optimization_barrier((prefix, intra))
+    return swap(prefix, ("zl", "core")).reshape(shape), intra, fetched
 
 
 def layer(tokens, norm_gain, w_qkv, head_gain, w_out):
     heads = w_qkv.shape[2] // HD
     reached, lower = earlier_masks()
     place = row_places(tokens.shape[0] * SIDE * SIDE)
-    columns = w_out[:, : w_out.shape[1] // FETCHED]
     own, reached, lower, place, slots = lax.optimization_barrier(
         (tokens, reached, lower, place, partner_slots())
     )
-    fetched = [columns] + [fetch(columns, ax, ay) for ax, ay in FLIPS]
     square = spread(own, SQUARES)
     gathered = spread(norm_rows(square, norm_gain), CROSSES)
     proj = [
@@ -144,15 +172,18 @@
             for k, v in zip(keys, values)
         ]
     )
-    prefix, gains = lax.optimization_barrier((earlier_sum(state, reached, lower), head_gain))
     causal = place[:, None] >= place[None, :]
-    outs = []
+    intra = []
     for h in range(heads):
         scores = jnp.einsum("td,sd->ts", query[h], keys[h], preferred_element_type=jnp.float32)
         scores = jnp.where(causal, scores, 0.0).astype(jnp.bfloat16)
-        attended = jnp.dot(scores, values[h], preferred_element_type=jnp.float32) + jnp.dot(
-            query[h], prefix[h], preferred_element_type=jnp.float32
-        )
+        intra.append(jnp.dot(scores, values[h], preferred_element_type=jnp.float32))
+    prefix, intra, fetched = earlier_sum(state, reached, lower, intra, w_out)
+    prefix, gains = lax.optimization_barrier((prefix, head_gain))
+    outs = []
+    for h in range(heads):
+        inter = jnp.dot(query[h], prefix[h], preferred_element_type=jnp.float32)
+        attended = intra[h] + inter
         scale = lax.rsqrt(jnp.mean(attended * attended, axis=-1, keepdims=True) + 1e-05)
         outs.append((attended * scale * gains[h * HD : (h + 1) * HD]).astype(jnp.bfloat16))
     head_out = jnp.concatenate(outs, axis=1)

time: 165 us -> 168 us (1.018)
  blocking collectives: 111 us -> 77.3 us
  waiting for transfers between devices: 18.8 us -> 40.1 us
  starting transfers between devices: 17.4 us -> 31.1 us
  Pallas kernels: 0 us -> 5.14 us
  matrix products: 9.11 us -> 5.73 us
    all_to_all x6 -> x5, blocking collectives: 111 us -> 77.3 us  [swap(): lax.all_to_all(value, axes, split_axis=0, concat_axis=0, tiled=True, axis...]
    all_to_all x1 -> x2, waiting for transfers between devices: 0.01 us -> 22.6 us  [swap(): lax.all_to_all(value, axes, split_axis=0, concat_axis=0, tiled=True, axis...]
    all_to_all x1 -> x2, starting transfers between devices: 5.81 us -> 20.7 us  [swap(): lax.all_to_all(value, axes, split_axis=0, concat_axis=0, tiled=True, axis...]
    pallas_call x0 -> x1, Pallas kernels: none -> 5.14 us  [products(): pl.pallas_call(products_kernel, out_shape=jax.ShapeDtypeStruct((heads.sha...]
    dot_general x8 -> x4, matrix products: 6.09 us -> 2.72 us  [the longest x2 1.4 us: layer(): inter = jnp.dot(query[h], prefix[h], preferred_element_type=jnp.float32)]
  transfers between devices with their start and end apart: 4 -> 5, of which waited for: 2 -> 4; matrix products, arithmetic and copies ran while one was open for 3% -> 2% of each run, Pallas kernels for 0% -> 0%
where the time goes in v7:
time: 168 us; the launch traced here: 166 us
  blocking collectives  77.3 us (46%)
  waiting for transfers between devices  40.1 us (24%)
  starting transfers between devices  31.1 us (19%)
  matrix products  5.73 us (3%)
  Pallas kernels  5.14 us (3%)
  other arithmetic  3.98 us (2%)
  local copies, waits for them, and re-layouts  2.75 us (2%)
    all_to_all x5, blocking collectives, swap(): lax.all_to_all(value, axes, split_axis=0, concat_axis=0, tiled=True, axis...  77.3 us
    all_to_all x2, waiting for transfers between devices, swap(): lax.all_to_all(value, axes, split_axis=0, concat_axis=0, tiled=True, axis...  22.6 us
    all_to_all x2, starting transfers between devices, swap(): lax.all_to_all(value, axes, split_axis=0, concat_axis=0, tiled=True, axis...  20.7 us
    ppermute x3, waiting for transfers between devices, fetch(): return lax.ppermute(value, PLANE, pairs)  17.5 us
    ppermute x3, starting transfers between devices, fetch(): return lax.ppermute(value, PLANE, pairs)  10.4 us
    pallas_call x1, Pallas kernels, products(): pl.pallas_call(products_kernel, out_shape=jax.ShapeDtypeStruct((heads.sha...  5.14 us
  transfers between devices with their start and end apart: 5, of which 4 were waited for; matrix products, arithmetic and copies ran while one was open for 2% of the time, Pallas kernels for 0%

profile of v7, /device:TPU:24, one launch (start us, length us, event | category | flops | bytes accessed | tf_op | source)
XLA Modules:
  0.0 166.4 jit_solution(9071672427842581303)
XLA Ops:
  0.1 0.7 pad_add_fusion.slots_ref
  0.8 0.9 broadcast_in_dim.10
  1.7 24.8 %all_to_all.35 = bf16[4,16,4096]{2,1,0:T(8,128)(2,1)S(1)} all-to-all(bf16[4,16,4096]{2,1,0:T(8,128)(2,1)S(1)} %broadcast_in_dim.10), channel_id=1, replica_groups={{1,2,5,6},{3,0,7,4},{9,10,13,14},{11,8,15,12},{20,21,24,25},{22,23,26,2..., dimensions={0} | all-to-all | bytes 1048576 | tf_op jit(solution)/shard_map/all_to_all | solution.py:54
  27.3 19.0 %all_to_all.36 = bf16[4,64,4096]{2,1,0:T(8,128)(2,1)S(1)} all-to-all(bf16[4,64,4096]{2,1,0:T(8,128)(2,1)S(1)} %broadcast_in_dim.11), channel_id=1, replica_groups={{1,0,13,12},{2,3,14,15},{5,4,9,8},{6,7,10,11},{20,23,16,19},{21,22,17,1..., dimensions={0} | all-to-all | bytes 4194304 | tf_op jit(solution)/shard_map/all_to_all | solution.py:54
  46.4 0.7 fusion.17
  47.1 0.7 fusion.14
  47.8 0.7 fusion.11
  49.0 8.4 %all_to_all.37 = bf16[8,32,128]{2,1,0:T(8,128)(2,1)S(1)} all-to-all(bf16[8,32,128]{2,1,0:T(8,128)(2,1)S(1)} %bitcast.60), channel_id=1, replica_groups=mesh['zh'=8,'zl'=4,'core'=2,'x'=4,'y'=4] {'zl','core'}, dimensions={0} | all-to-all | bytes 131072 | tf_op jit(solution)/shard_map/all_to_all | solution.py:54
  58.1 16.8 %all-to-all-start.3 = ((bf16[8,32,128]{2,1,0:T(8,128)(2,1)}), bf16[8,32,128]{2,1,0:T(8,128)(2,1)S(1)}, u32[]{:S(2)}, u32[]{:S(2)}) async-start(bf16[8,32,128]{2,1,0:T(8,128)(2,1)} %broadcast_in_dim.12), calls=%async_computation.3 | async-start | bytes 131072 | tf_op jit(solution)/shard_map/all_to_all | solution.py:54
  75.2 1.0 fusion.20
  76.2 22.6 %all-to-all-done.3 = bf16[8,32,128]{2,1,0:T(8,128)(2,1)S(1)} async-done(((bf16[8,32,128]{2,1,0:T(8,128)(2,1)}), bf16[8,32,128]{2,1,0:T(8,128)(2,1)S(1)}, u32[]{:S(2)}, u32[]{:S(2)}) %all-to-all-start.3) | async-done | bytes 65568 | tf_op jit(solution)/shard_map/all_to_all | solution.py:54
  99.5 3.9 %all-to-all-start.4 = ((bf16[8,32,128]{2,1,0:T(8,128)(2,1)}), bf16[8,32,128]{2,1,0:T(8,128)(2,1)S(1)}, u32[]{:S(2)}, u32[]{:S(2)}) async-start(bf16[8,32,128]{2,1,0:T(8,128)(2,1)} %add_convert_fusion.1), calls=%async_computation.4 | async-start | bytes 131072 | tf_op jit(solution)/shard_map/all_to_all | solution.py:54
  103.6 3.4 %collective-permute-start.2 = (bf16[256,2048]{1,0:T(8,128)(2,1)S(1)}, bf16[256,2048]{1,0:T(8,128)(2,1)}, u32[]{:S(2)}, u32[]{:S(2)}) collective-permute-start(bf16[256,2048]{1,0:T(8,128)(2,1)S(1)} %slice.67.refs_0_), channel_id=1, source_target_pairs={{1,12},{0,13},{13,0},{12,1},{2,15},{3,14},{14,3},{15,2},{5,8},{4,9... | collective-permute-start | bytes 3145736 | tf_op jit(solution)/shard_map/ppermute | solution.py:43
  106.9 4.2 %collective-permute-start.1 = (bf16[256,2048]{1,0:T(8,128)(2,1)S(1)}, bf16[256,2048]{1,0:T(8,128)(2,1)}, u32[]{:S(2)}, u32[]{:S(2)}) collective-permute-start(bf16[256,2048]{1,0:T(8,128)(2,1)S(1)} %slice.67.refs_0_), channel_id=1, source_target_pairs={{1,13},{0,12},{13,1},{12,0},{2,14},{3,15},{14,2},{15,3},{5,9},{4,8... | collective-permute-start | bytes 3145736 | tf_op jit(solution)/shard_map/ppermute | solution.py:43
  111.2 2.8 %collective-permute-start = (bf16[256,2048]{1,0:T(8,128)(2,1)S(1)}, bf16[256,2048]{1,0:T(8,128)(2,1)}, u32[]{:S(2)}, u32[]{:S(2)}) collective-permute-start(bf16[256,2048]{1,0:T(8,128)(2,1)S(1)} %slice.67.refs_0_), channel_id=1, source_target_pairs={{1,0},{0,1},{13,12},{12,13},{2,3},{3,2},{14,15},{15,14},{5,4},{4,5... | collective-permute-start | bytes 3145736 | tf_op jit(solution)/shard_map/ppermute | solution.py:43
  114.0 1.2 multiply_reduce_fusion.2
  116.2 6.4 %collective-permute-done.2.refs_3_ = bf16[256,2048]{1,0:T(8,128)(2,1)} collective-permute-done((bf16[256,2048]{1,0:T(8,128)(2,1)S(1)}, bf16[256,2048]{1,0:T(8,128)(2,1)}, u32[]{:S(2)}, u32[]{:S(2)}) %collective-permute-start.2) | collective-permute-done | bytes 1048608 | tf_op jit(solution)/shard_map/ppermute | solution.py:43
  122.6 10.8 %collective-permute-done.1.refs_2_ = bf16[256,2048]{1,0:T(8,128)(2,1)} collective-permute-done((bf16[256,2048]{1,0:T(8,128)(2,1)S(1)}, bf16[256,2048]{1,0:T(8,128)(2,1)}, u32[]{:S(2)}, u32[]{:S(2)}) %collective-permute-start.1) | collective-permute-done | bytes 1048608 | tf_op jit(solution)/shard_map/ppermute | solution.py:43
  133.7 14.3 %all_to_all.38 = bf16[4,64,2304]{2,1,0:T(8,128)(2,1)S(1)} all-to-all(bf16[4,64,2304]{2,1,0:T(8,128)(2,1)S(1)} %bitcast.55), channel_id=1, replica_groups={{1,0,13,12},{2,3,14,15},{5,4,9,8},{6,7,10,11},{20,23,16,19},{21,22,17,1..., dimensions={0} | all-to-all | bytes 2359296 | tf_op jit(solution)/shard_map/all_to_all | solution.py:54
  148.0 0.7 slice.69.heads_ref
  148.6 5.1 %products.1 = bf16[64,2048]{1,0:T(8,128)(2,1)} custom-call(s32[4]{0:T(128)} %pad_add_fusion.slots_ref, bf16[4,64,256]{2,1,0:T(8,128)(2,1)} %slice.69.heads_ref, bf16[256,2048]{1,0:T(8,128)(2,1)} %copy-done, bf16[256,2048]{1,0:T(8,128)(2,1)} %collective-permute-done.refs_1_, bf16[256,2048]{1,0:T(8,128)(2,1)} %collective-permute-done.1.refs_2_, ...), custom_call_target="tpu_custom_call" | custom-call | tf_op jit(solution)/shard_map/products/pallas_call | solution.py:92
  153.9 1.0 pad_maximum_fusion.1
  154.9 10.7 %all_to_all.39 = bf16[4,16,4096]{2,1,0:T(8,128)(2,1)S(1)} all-to-all(bf16[4,16,4096]{2,1,0:T(8,128)(2,1)S(1)} %bitcast.59), channel_id=1, replica_groups={{1,2,5,6},{3,0,7,4},{9,10,13,14},{11,8,15,12},{20,21,24,25},{22,23,26,2..., dimensions={0} | all-to-all | bytes 1048576 | tf_op jit(solution)/shard_map/all_to_all | solution.py:54
  165.6 0.7 fusion.30
  (41 shorter events, 4.4 us)
Async XLA Ops:
  0.0 26.9 %copy-start.3 = (f32[4096]{0:T(1024)S(1)}, f32[4096]{0:T(1024)}, u32[]{:S(2)}) copy-start(f32[4096]{0:T(1024)} %param.6) | copy-start | bytes 49156
  27.1 19.3 %copy-start.5 = (bf16[4096,3,256]{2,0,1:T(8,128)(2,1)S(1)}, bf16[4096,3,256]{2,0,1:T(8,128)(2,1)}, u32[]{:S(2)}) copy-start(bf16[4096,3,256]{2,0,1:T(8,128)(2,1)} %param.7) | copy-start | bytes 18874372
  48.6 54.9 %copy-start.1 = (bf16[256,4096]{1,0:T(8,128)(2,1)S(1)}, bf16[256,4096]{1,0:T(8,128)(2,1)}, u32[]{:S(2)}) copy-start(bf16[256,4096]{1,0:T(8,128)(2,1)} %param.9) | copy-start | bytes 6291460
  57.4 56.6 %copy-start.4 = (f32[256]{0:T(256)S(1)}, f32[256]{0:T(256)}, u32[]{:S(2)}) copy-start(f32[256]{0:T(256)} %param.8) | copy-start | bytes 3076
  58.1 40.7 %all-to-all-start.3 = ((bf16[8,32,128]{2,1,0:T(8,128)(2,1)}), bf16[8,32,128]{2,1,0:T(8,128)(2,1)S(1)}, u32[]{:S(2)}, u32[]{:S(2)}) async-start(bf16[8,32,128]{2,1,0:T(8,128)(2,1)} %broadcast_in_dim.12), calls=%async_computation.3 | async-start | bytes 131072 | tf_op jit(solution)/shard_map/all_to_all | solution.py:54
  99.5 14.5 %all-to-all-start.4 = ((bf16[8,32,128]{2,1,0:T(8,128)(2,1)}), bf16[8,32,128]{2,1,0:T(8,128)(2,1)S(1)}, u32[]{:S(2)}, u32[]{:S(2)}) async-start(bf16[8,32,128]{2,1,0:T(8,128)(2,1)} %add_convert_fusion.1), calls=%async_computation.4 | async-start | bytes 131072 | tf_op jit(solution)/shard_map/all_to_all | solution.py:54
  103.6 12.6 %copy-start = (bf16[256,2048]{1,0:T(8,128)(2,1)}, bf16[256,2048]{1,0:T(8,128)(2,1)S(1)}, u32[]{:S(2)}) copy-start(bf16[256,2048]{1,0:T(8,128)(2,1)S(1)} %slice.67.refs_0_) | copy-start | bytes 3145732
  103.6 19.0 %collective-permute-start.2 = (bf16[256,2048]{1,0:T(8,128)(2,1)S(1)}, bf16[256,2048]{1,0:T(8,128)(2,1)}, u32[]{:S(2)}, u32[]{:S(2)}) collective-permute-start(bf16[256,2048]{1,0:T(8,128)(2,1)S(1)} %slice.67.refs_0_), channel_id=1, source_target_pairs={{1,12},{0,13},{13,0},{12,1},{2,15},{3,14},{14,3},{15,2},{5,8},{4,9... | collective-permute-start | bytes 3145736 | tf_op jit(solution)/shard_map/ppermute | solution.py:43
  106.9 26.5 %collective-permute-start.1 = (bf16[256,2048]{1,0:T(8,128)(2,1)S(1)}, bf16[256,2048]{1,0:T(8,128)(2,1)}, u32[]{:S(2)}, u32[]{:S(2)}) collective-permute-start(bf16[256,2048]{1,0:T(8,128)(2,1)S(1)} %slice.67.refs_0_), channel_id=1, source_target_pairs={{1,13},{0,12},{13,1},{12,0},{2,14},{3,15},{14,2},{15,3},{5,9},{4,8... | collective-permute-start | bytes 3145736 | tf_op jit(solution)/shard_map/ppermute | solution.py:43
  111.2 22.5 %collective-permute-start = (bf16[256,2048]{1,0:T(8,128)(2,1)S(1)}, bf16[256,2048]{1,0:T(8,128)(2,1)}, u32[]{:S(2)}, u32[]{:S(2)}) collective-permute-start(bf16[256,2048]{1,0:T(8,128)(2,1)S(1)} %slice.67.refs_0_), channel_id=1, source_target_pairs={{1,0},{0,1},{13,12},{12,13},{2,3},{3,2},{14,15},{15,14},{5,4},{4,5... | collective-permute-start | bytes 3145736 | tf_op jit(solution)/shard_map/ppermute | solution.py:43
  153.8 11.9 %copy-start.2 = (bf16[16,4096]{1,0:T(8,128)(2,1)S(1)}, bf16[16,4096]{1,0:T(8,128)(2,1)}, u32[]{:S(2)}) copy-start(bf16[16,4096]{1,0:T(8,128)(2,1)} %param.5) | copy-start | bytes 393220

commit v8 on v6

--- a/solution.py
+++ b/solution.py
@@ -88,11 +88,8 @@
     own, reached, lower, place = lax.optimization_barrier((tokens, reached, lower, place))
     square = spread(own, SQUARES)
     gathered = spread(norm_rows(square, norm_gain), CROSSES)
-    proj = [
-        jnp.dot(gathered, w_qkv[:, j], preferred_element_type=jnp.float32).astype(jnp.bfloat16)
-        for j in range(3)
-    ]
-    proj = lax.optimization_barrier(proj)
+    flat = jnp.einsum("tk,kjn->jtn", gathered, w_qkv, preferred_element_type=jnp.float32)
+    proj = lax.optimization_barrier(flat.astype(jnp.bfloat16))
     query, keys, values = [[p[:, h * HD : (h + 1) * HD] for h in range(heads)] for p in proj]
     state = jnp.stack(
         [

time: 141 us -> 140 us (level)
  no operation moved by 1% of the time
where the time goes in v8:
time: 140 us
  blocking collectives  132 us (94%)
  matrix products  4.12 us (3%)
  other arithmetic  1.69 us (1%)
  local copies, waits for them, and re-layouts  1.53 us (1%)
    all_to_all x7, blocking collectives, swap(): lax.all_to_all(value, axes, split_axis=0, concat_axis=0, tiled=True, axis...  132 us

profile of v8, /device:TPU:24, one launch (start us, length us, event | category | flops | bytes accessed | tf_op | source)
XLA Modules:
  0.0 139.8 jit_solution(13173206273691853045)
XLA Ops:
  0.1 1.1 broadcast_in_dim.10
  1.2 24.9 %all_to_all.35 = bf16[4,16,4096]{2,1,0:T(8,128)(2,1)S(1)} all-to-all(bf16[4,16,4096]{2,1,0:T(8,128)(2,1)S(1)} %broadcast_in_dim.10), channel_id=1, replica_groups={{1,2,5,6},{3,0,7,4},{9,10,13,14},{11,8,15,12},{20,21,24,25},{22,23,26,2..., dimensions={0} | all-to-all | bytes 1048576 | tf_op jit(solution)/shard_map/all_to_all | solution.py:29
  26.1 0.2 multiply_reduce_fusion.1
  26.2 0.1 rsqrt.28
  26.3 0.2 fusion.10
  26.6 0.2 broadcast_in_dim.11
  26.8 19.0 %all_to_all.36 = bf16[4,64,4096]{2,1,0:T(8,128)(2,1)S(1)} all-to-all(bf16[4,64,4096]{2,1,0:T(8,128)(2,1)S(1)} %broadcast_in_dim.11), channel_id=1, replica_groups={{1,0,13,12},{2,3,14,15},{5,4,9,8},{6,7,10,11},{20,23,16,19},{21,22,17,1..., dimensions={0} | all-to-all | bytes 4194304 | tf_op jit(solution)/shard_map/all_to_all | solution.py:29
  45.8 1.8 %fusion = bf16[3,256,256]{2,1,0:T(8,128)(2,1)S(1)} fusion(bf16[256,4096,1]{1,0,2:T(8,128)(2,1)S(1)} %bitcast.42, bf16[4096,3,256]{2,0,1:T(8,128)(2,1)S(1)} %copy-done.4), kind=kOutput, calls=%fused_computation.2 | convolution fusion | flops 1610809344 | bytes 8781824 | tf_op jit(solution)/shard_map/tk,kjn->jtn/dot_general | solution.py:91
  47.7 0.2 fusion.7
  47.9 0.2 fusion.8
  48.1 8.3 %all_to_all.37 = bf16[8,32,128]{2,1,0:T(8,128)(2,1)S(1)} all-to-all(bf16[8,32,128]{2,1,0:T(8,128)(2,1)S(1)} %bitcast.45), channel_id=1, replica_groups=mesh['zh'=8,'zl'=4,'core'=2,'x'=4,'y'=4] {'zl','core'}, dimensions={0} | all-to-all | bytes 131072 | tf_op jit(solution)/shard_map/all_to_all | solution.py:29
  56.4 0.1 multiply_reduce_fusion
  56.5 40.5 %all_to_all.38 = bf16[8,32,128]{2,1,0:T(8,128)(2,1)S(1)} all-to-all(bf16[8,32,128]{2,1,0:T(8,128)(2,1)S(1)} %broadcast_in_dim.13), channel_id=1, replica_groups=mesh['zh'=8,'zl'=4,'core'=2,'x'=4,'y'=4] {'zh'}, dimensions={0} | all-to-all | bytes 131072 | tf_op jit(solution)/shard_map/all_to_all | solution.py:29
  97.0 9.7 %all_to_all.39 = bf16[8,32,128]{2,1,0:T(8,128)(2,1)S(1)} all-to-all(bf16[8,32,128]{2,1,0:T(8,128)(2,1)S(1)} %add_convert_fusion.1), channel_id=1, replica_groups=mesh['zh'=8,'zl'=4,'core'=2,'x'=4,'y'=4] {'zl','core'}, dimensions={0} | all-to-all | bytes 131072 | tf_op jit(solution)/shard_map/all_to_all | solution.py:29
  106.7 0.2 fusion.23
  106.9 0.2 fusion.37
  107.2 0.4 multiply_reduce_fusion.2
  107.6 0.4 multiply_reduce_fusion.3
  108.0 0.1 multiply_convert_fusion
  108.1 0.7 convolution_convert_fusion
  108.8 19.2 %all_to_all.40 = bf16[4,64,4096]{2,1,0:T(8,128)(2,1)S(1)} all-to-all(bf16[4,64,4096]{2,1,0:T(8,128)(2,1)S(1)} %bitcast.40), channel_id=1, replica_groups={{1,0,13,12},{2,3,14,15},{5,4,9,8},{6,7,10,11},{20,23,16,19},{21,22,17,1..., dimensions={0} | all-to-all | bytes 4194304 | tf_op jit(solution)/shard_map/all_to_all | solution.py:29
  128.1 0.3 add_convert_fusion
  128.3 10.7 %all_to_all.41 = bf16[4,16,4096]{2,1,0:T(8,128)(2,1)S(1)} all-to-all(bf16[4,16,4096]{2,1,0:T(8,128)(2,1)S(1)} %bitcast.41), channel_id=1, replica_groups={{1,2,5,6},{3,0,7,4},{9,10,13,14},{11,8,15,12},{20,21,24,25},{22,23,26,2..., dimensions={0} | all-to-all | bytes 1048576 | tf_op jit(solution)/shard_map/all_to_all | solution.py:29
  139.1 0.7 fusion.13
  (24 shorter events, 0.3 us)
Async XLA Ops:
  0.0 108.1 %copy-start = (bf16[256,4096]{1,0:T(8,128)(2,1)S(1)}, bf16[256,4096]{1,0:T(8,128)(2,1)}, u32[]{:S(2)}) copy-start(bf16[256,4096]{1,0:T(8,128)(2,1)} %param.9) | copy-start | bytes 6291460
  0.0 26.3 %copy-start.2 = (f32[4096]{0:T(1024)S(1)}, f32[4096]{0:T(1024)}, u32[]{:S(2)}) copy-start(f32[4096]{0:T(1024)} %param.6) | copy-start | bytes 49156
  26.6 19.3 %copy-start.4 = (bf16[4096,3,256]{2,0,1:T(8,128)(2,1)S(1)}, bf16[4096,3,256]{2,0,1:T(8,128)(2,1)}, u32[]{:S(2)}) copy-start(bf16[4096,3,256]{2,0,1:T(8,128)(2,1)} %param.7) | copy-start | bytes 18874372
  47.7 59.5 %copy-start.3 = (f32[256]{0:T(256)S(1)}, f32[256]{0:T(256)}, u32[]{:S(2)}) copy-start(f32[256]{0:T(256)} %param.8) | copy-start | bytes 3076
  128.1 11.0 %copy-start.1 = (bf16[16,4096]{1,0:T(8,128)(2,1)S(1)}, bf16[16,4096]{1,0:T(8,128)(2,1)}, u32[]{:S(2)}) copy-start(bf16[16,4096]{1,0:T(8,128)(2,1)} %param.5) | copy-start | bytes 393220
